TPU v7x, 32 devices: a whole 2x2x4 slice. The times are simulated.
32 devices in a mesh: freq: 8 (over y, x, core), tile: 4 (over z).
Axes of the slice: x: 2, y: 2, z: 4, core: 2. Of those that a mesh axis runs over, the one named last changes fastest.
Arguments:
- left_factor: bfloat16 [128, 8, 32, 2, 16, 256], P('freq', 'tile'), may hold values from -1.5 to 1.5
- right_factor: bfloat16 [128, 8, 32, 2, 16, 256], P('freq', None, 'tile'), may hold values from -0.0625 to 0.0625
- tile_ranks: int32 [128, 8, 32], P('freq'), may hold values from 1 to 16
- tile_scales: float32 [128, 2, 8, 32], P('freq'), may hold values from 0.5 to 2
- recorded: float32 [128, 2, 8, 2048], P('freq', None, None, 'tile'), may hold values from -12 to 12
- step_sizes: float32 [128], P('freq'), may hold values from 0.2 to 0.6
- thresholds: float32 [8], replicated, may hold values from 0.1 to 0.5
Outputs:
- estimate: float32 [128, 2, 8, 8192], P('freq', None, None, 'tile')
Inputs may be any that keep to these rules, and one draw needn't show every extreme that they name: `tile_ranks`: rank of each tile; rank slots at and above it carry no weight.
All inputs are finite; a program needn't handle non-finite values.
Results may differ from a plain program's by a relative error of at most 0.0058.
Values may be sent and summed in bfloat16 or wider, within the bound.
A program may use at most 128 MiB of HBM per device.

v0:
```python
import math

import jax
import jax.numpy as jnp
from jax import lax
from jax.sharding import PartitionSpec as P

F = 128


def dft_tables(freq_index, time_count):
    times_row = jnp.arange(time_count, dtype=jnp.int32)
    phase_steps = (freq_index[:, None] * times_row[None, :] % time_count).astype(jnp.float32)
    angles = phase_steps * (2.0 * math.pi / time_count)
    scaling = jnp.where(
        freq_index == 0, math.sqrt(1.0 / time_count), math.sqrt(2.0 / time_count)
    ).astype(jnp.float32)
    return (scaling[:, None] * jnp.cos(angles), scaling[:, None] * jnp.sin(angles))


def slot_weights(tile_ranks, tile_scales, rank_max):
    slot_index = jnp.arange(rank_max, dtype=jnp.int32)
    live_slots = (slot_index < tile_ranks[..., None]).astype(jnp.float32)
    return (tile_scales[:, 0] * tile_scales[:, 1])[..., None] * live_slots


def per_device(
    left_factor, right_factor, tile_ranks, tile_scales, recorded, step_sizes, thresholds
):
    freqs_here = left_factor.shape[0]
    rows_here = left_factor.shape[1]
    col_tiles = left_factor.shape[2]
    rank_max = left_factor.shape[4]
    tile_width = left_factor.shape[5]
    row_tiles = right_factor.shape[1]
    cols_here = right_factor.shape[2]
    virtual = recorded.shape[2]
    tile_pos = lax.axis_index("tile")
    columns_here = cols_here * tile_width
    time_count = 2 * F
    highest = lax.Precision.HIGHEST
    weights = slot_weights(tile_ranks, tile_scales, rank_max)
    weights_right = lax.dynamic_slice_in_dim(weights, tile_pos * cols_here, cols_here, 2)
    weights_left = lax.dynamic_slice_in_dim(weights, tile_pos * rows_here, rows_here, 1)
    left_real = left_factor[:, :, :, 0]
    left_imag = left_factor[:, :, :, 1]
    right_real = right_factor[:, :, :, 0]
    right_imag = right_factor[:, :, :, 1]
    cos_all, sin_all = dft_tables(jnp.arange(F, dtype=jnp.int32), time_count)

    def gradient(residual):
        halves = residual.astype(jnp.bfloat16).reshape(
            freqs_here, 2, virtual, rows_here, tile_width
        )

        def contract_left(matrix, vectors):
            return jnp.einsum(
                "fijkq,fviq->fijkv", matrix, vectors, preferred_element_type=jnp.float32
            )

        dual_real = contract_left(left_real, halves[:, 0]) + contract_left(left_imag, halves[:, 1])
        dual_imag = contract_left(left_real, halves[:, 1]) - contract_left(left_imag, halves[:, 0])
        duals = (
            jnp.stack([dual_real, dual_imag], 3) * weights_left[:, :, :, None, :, None]
        ).astype(jnp.bfloat16)
        duals = duals.reshape(freqs_here, rows_here, col_tiles, 2, rank_max * virtual)
        arrived = lax.all_to_all(duals, "tile", split_axis=2, concat_axis=1, tiled=True)
        arrived = arrived.reshape(freqs_here, row_tiles, cols_here, 2, rank_max, virtual)

        def spread(matrix, vectors):
            return jnp.einsum(
                "fijkp,fijkv->fvjp", matrix, vectors, preferred_element_type=jnp.float32
            )

        grad_real = spread(right_real, arrived[:, :, :, 0]) - spread(
            right_imag, arrived[:, :, :, 1]
        )
        grad_imag = spread(right_real, arrived[:, :, :, 1]) + spread(
            right_imag, arrived[:, :, :, 0]
        )
        return jnp.stack([grad_real, grad_imag], 1).reshape(freqs_here, 2, virtual, columns_here)

    def to_time(wavefield):
        swapped = lax.all_to_all(wavefield, "freq", split_axis=3, concat_axis=0, tiled=True)
        return jnp.einsum("fvn,ft->nvt", swapped[:, 0], cos_all, precision=highest) - jnp.einsum(
            "fvn,ft->nvt", swapped[:, 1], sin_all, precision=highest
        )

    def shrink(signal):
        excess = jnp.abs(signal) - thresholds[None, :, None]
        return jnp.sign(signal) * jnp.maximum(excess, 0.0)

    def to_freq(signal):
        real_part = jnp.einsum("nvt,ft->fvn", signal, cos_all, precision=highest)
        imag_part = -jnp.einsum("nvt,ft->fvn", signal, sin_all, precision=highest)
        return lax.all_to_all(
            jnp.stack([real_part, imag_part], 1), "freq", split_axis=0, concat_axis=3, tiled=True
        )

    scaled = step_sizes[:, None, None, None]
    first = to_freq(shrink(to_time(scaled * gradient(recorded))))
    halves = first.astype(jnp.bfloat16).reshape(freqs_here, 2, virtual, cols_here, tile_width)

    def project(matrix, vectors):
        return jnp.einsum("fijkp,fvjp->fijkv", matrix, vectors, preferred_element_type=jnp.float32)

    coef_real = project(right_real, halves[:, 0]) + project(right_imag, halves[:, 1])
    coef_imag = project(right_real, halves[:, 1]) - project(right_imag, halves[:, 0])
    coeffs = (jnp.stack([coef_real, coef_imag], 3) * weights_right[:, :, :, None, :, None]).astype(
        jnp.bfloat16
    )
    coeffs = coeffs.reshape(freqs_here, row_tiles, cols_here, 2, rank_max * virtual)
    arrived = lax.all_to_all(coeffs, "tile", split_axis=1, concat_axis=2, tiled=True)
    arrived = arrived.reshape(freqs_here, rows_here, col_tiles, 2, rank_max, virtual)

    def expand(matrix, vectors):
        return jnp.einsum("fijkq,fijkv->fviq", matrix, vectors, preferred_element_type=jnp.float32)

    image_real = expand(left_real, arrived[:, :, :, 0]) - expand(left_imag, arrived[:, :, :, 1])
    image_imag = expand(left_real, arrived[:, :, :, 1]) + expand(left_imag, arrived[:, :, :, 0])
    return to_freq(
        shrink(
            to_time(
                first
                + scaled
                * gradient(
                    recorded
                    - jnp.stack([image_real, image_imag], 1).reshape(
                        freqs_here, 2, virtual, rows_here * tile_width
                    )
                )
            )
        )
    )


def solution(mesh):
    return jax.shard_map(
        per_device,
        mesh=mesh,
        in_specs=(
            P("freq", "tile", None, None, None, None),
            P("freq", None, "tile", None, None, None),
            P("freq", None, None),
            P("freq", None, None, None),
            P("freq", None, None, "tile"),
            P("freq"),
            P(),
        ),
        out_specs=P("freq", None, None, "tile"),
        check_vma=False,
    )
```

profile of v0, /device:TPU:0, one launch (start us, length us, event | category | flops | bytes accessed | tf_op | source)
XLA Modules:
  0.0 608.5 jit_solution(13973984493373626342)
XLA Ops:
  6.1 13.4 %fusion.145 = f32[16,2,32,16,8]{3,4,2,1,0:T(8,128)S(1)} fusion(bf16[16,1,8,2,256]{4,3,2,1,0:T(2,128)(2,1)S(1)} %get-tuple-element.17, bf16[16,2,32,2,16,256]{5,4,3,2,1,0:T(8,128)(2,1)} %param.7), kind=kOutput, calls=%fused_computation.132 | convolution fusion | flops 67108864 | bytes 9043968 | tf_op jit(solution)/shard_map/fijkq,fviq->fijkv/dot_general | solution.py:57
  19.5 15.4 %fusion.146 = f32[16,2,32,16,8]{3,4,2,1,0:T(8,128)} fusion(bf16[16,1,8,2,256]{4,3,2,1,0:T(2,128)(2,1)S(1)} %get-tuple-element.18, bf16[16,2,32,2,16,256]{5,4,3,2,1,0:T(8,128)(2,1)} %param.7), kind=kOutput, calls=%fused_computation.133 | convolution fusion | flops 67108864 | bytes 9043968 | tf_op jit(solution)/shard_map/fijkq,fviq->fijkv/dot_general | solution.py:57
  34.9 15.8 %convolution_add_fusion = f32[16,2,32,16,8]{3,4,2,1,0:T(8,128)} fusion(f32[16,2,32,16,8]{3,4,2,1,0:T(8,128)S(1)} %fusion.145, bf16[16,1,8,2,256]{4,3,2,1,0:T(2,128)(2,1)S(1)} %get-tuple-element.18, bf16[16,2,32,2,16,256]{5,4,3,2,1,0:T(8,128)(2,1)} %param.7), kind=kOutput, calls=%fused_computation.36 | convolution fusion | flops 67239936 | bytes 9568256 | tf_op jit(solution)/shard_map/fijkq,fviq->fijkv/dot_general | solution.py:57
  50.7 2.9 copy.395
  54.2 16.5 %convolution_subtract_fusion = f32[16,2,32,16,8]{3,4,2,1,0:T(8,128)} fusion(f32[16,2,32,16,8]{3,4,2,1,0:T(8,128)} %fusion.146, bf16[16,1,8,2,256]{4,3,2,1,0:T(2,128)(2,1)S(1)} %get-tuple-element.17, bf16[16,2,32,2,16,256]{5,4,3,2,1,0:T(8,128)(2,1)} %param.7), kind=kOutput, calls=%fused_computation.35 | convolution fusion | flops 67239936 | bytes 13238272 | tf_op jit(solution)/shard_map/fijkq,fviq->fijkv/dot_general | solution.py:57
  70.7 2.9 copy.396
  77.4 6.5 %all-to-all-start = ((bf16[16,2,32,2,128]{4,0,3,1,2:T(8,128)(2,1)}), bf16[16,2,32,2,128]{4,0,3,1,2:T(8,128)(2,1)S(1)}, u32[]{:S(2)}, u32[]{:S(2)}) async-start(bf16[16,2,32,2,128]{4,0,3,1,2:T(8,128)(2,1)} %copy.403), calls=%async_computation | async-start | bytes 1048576 | tf_op jit(solution)/shard_map/all_to_all | solution.py:67
  83.9 11.9 %fusion.195 = (bf16[16,8,8,1,16,256]{5,4,3,2,1,0:T(8,128)(2,1)}, bf16[16,8,8,1,16,256]{5,4,3,2,1,0:T(8,128)(2,1)}) fusion(bf16[16,8,8,2,16,256]{5,4,3,2,1,0:T(8,128)(2,1)} %param.8), kind=kLoop, calls=%fused_computation.178 | loop fusion | bytes 33554432 | tf_op jit(solution)/shard_map/slice | solution.py:47
  95.8 2.6 all-to-all-done
  98.4 3.1 copy.405
  101.4 4.9 fusion.198
  106.3 5.7 copy.497
  112.0 6.0 copy.495
  118.1 6.2 %fusion.71 = f32[16,8,8,256]{3,2,1,0:T(8,128)S(1)} fusion(bf16[16,8,8,1,16,256]{5,4,3,2,1,0:T(8,128)(2,1)} %get-tuple-element.8, bf16[16,8,8,1,16,8]{4,5,1,2,0,3:T(8,128)(2,1)} %copy.495), kind=kOutput, calls=%fused_computation.73 | convolution fusion | flops 67108864 | bytes 9699328 | tf_op jit(solution)/shard_map/fijkp,fijkv->fvjp/dot_general | solution.py:71
  124.3 5.6 fusion.68
  134.5 11.4 %copy.410 = f32[16,2,8,2048]{0,2,1,3:T(8,128)} copy(f32[16,2,8,2048]{3,2,1,0:T(8,128)S(1)} %maximum_multiply_fusion.1) | data formatting | bytes 4194304 | tf_op jit(solution)/shard_map/mul | solution.py:101
  145.9 11.6 %reshape.101 = f32[8,1,65536]{2,1,0:T(1,128)} reshape(f32[2048,2,8,16]{3,2,1,0:T(8,128)} %bitcast.366) | data formatting | bytes 4194304
  157.5 4.0 all-to-all-start.1
  161.5 26.6 %all-to-all-done.1 = f32[8,1,65536]{2,1,0:T(1,128)S(1)} async-done(((f32[8,1,65536]{2,1,0:T(1,128)}), f32[8,1,65536]{2,1,0:T(1,128)S(1)}, u32[]{:S(2)}, u32[]{:S(2)}) %all-to-all-start.1) | async-done | bytes 2097184 | tf_op jit(solution)/shard_map/all_to_all | solution.py:84
  190.0 7.2 %reduce = f32[8,65536]{1,0:T(8,128)S(1)} reduce(f32[8,1,65536]{2,1,0:T(1,128)} %copy-done.1, f32[]{:T(128)} %broadcast.71), dimensions={1}, to_apply=%all_to_all.88.reduce_sub_computation | reduce | bytes 4194308 | tf_op jit(solution)/shard_map/all_to_all | solution.py:84
  197.2 11.3 %reshape.102 = f32[2048,2,8,16]{3,2,1,0:T(8,128)} reshape(f32[8,65536]{1,0:T(8,128)S(1)} %reduce) | data formatting | bytes 4194304
  208.4 10.2 %copy.412 = f32[8,16,2,8,256]{4,1,0,3,2:T(8,128)S(1)} copy(f32[8,16,2,8,256]{1,3,2,4,0:T(8,128)} %bitcast.367) | data formatting | bytes 4194304 | tf_op jit(solution)/shard_map/all_to_all | solution.py:84
  220.9 3.1 maximum_multiply_fusion.4
  230.2 3.8 all-to-all-start.2
  237.6 22.8 %all-to-all-done.2 = f32[128,2,8,256]{3,2,1,0:T(8,128)S(1)} async-done(((f32[128,2,8,256]{3,2,1,0:T(8,128)}), f32[128,2,8,256]{3,2,1,0:T(8,128)S(1)}, u32[]{:S(2)}, u32[]{:S(2)}) %all-to-all-start.2) | async-done | bytes 2097184 | tf_op jit(solution)/shard_map/all_to_all | solution.py:96
  260.5 13.3 %fusion.18 = f32[16,8,8,8,16]{4,2,3,1,0:T(8,128)S(1)} fusion(bf16[16,8,8,1,16,256]{5,4,3,2,1,0:T(8,128)(2,1)} %get-tuple-element.7, bf16[16,2,8,8,256]{4,2,3,0,1:T(8,128)(2,1)S(1)} %bitcast.377), kind=kOutput, calls=%fused_computation.25 | convolution fusion | flops 67108864 | bytes 9437184 | tf_op jit(solution)/shard_map/fijkp,fvjp->fijkv/dot_general | solution.py:105
  273.9 11.7 %fusion.19 = f32[16,8,8,8,16]{4,2,3,1,0:T(8,128)} fusion(bf16[16,8,8,1,16,256]{5,4,3,2,1,0:T(8,128)(2,1)S(1)} %bitcast.357, bf16[16,2,8,8,256]{4,2,3,0,1:T(8,128)(2,1)S(1)} %bitcast.378), kind=kOutput, calls=%fused_computation.26 | convolution fusion | flops 67108864 | bytes 9437184 | tf_op jit(solution)/shard_map/fijkp,fvjp->fijkv/dot_general | solution.py:105
  285.6 12.3 %subtract_bitcast_fusion = f32[16,8,8,16,8]{3,4,1,2,0:T(8,128)} fusion(f32[16,8,8,8,16]{4,2,3,1,0:T(8,128)S(1)} %fusion.18, bf16[16,8,8,1,16,256]{5,4,3,2,1,0:T(8,128)(2,1)S(1)} %bitcast.363, bf16[16,2,8,8,256]{4,2,3,0,1:T(8,128)(2,1)S(1)} %bitcast.379), kind=kOutput, calls=%fused_computation.21 | convolution fusion | flops 67239936 | bytes 13631488 | tf_op jit(solution)/shard_map/fijkp,fvjp->fijkv/dot_general | solution.py:105
  297.9 6.0 copy.421
  304.0 16.4 %add_bitcast_fusion = f32[16,8,8,16,8]{3,4,1,2,0:T(8,128)} fusion(f32[16,8,8,8,16]{4,2,3,1,0:T(8,128)} %fusion.19, bf16[16,8,8,1,16,256]{5,4,3,2,1,0:T(8,128)(2,1)} %get-tuple-element.8, bf16[16,2,8,8,256]{4,2,3,0,1:T(8,128)(2,1)S(1)} %bitcast.380), kind=kOutput, calls=%fused_computation.22 | convolution fusion | flops 67239936 | bytes 9961472 | tf_op jit(solution)/shard_map/fijkp,fvjp->fijkv/dot_general | solution.py:105
  320.3 6.0 copy.420
  326.4 6.8 %maximum_multiply_fusion = bf16[16,8,8,2,128]{0,4,2,1,3:T(8,128)(2,1)} fusion(f32[16,8,8,1,128]{0,4,2,1,3:T(8,128)} %bitcast.375, f32[16,8,8,1,128]{0,4,2,1,3:T(8,128)} %bitcast.376, f32[16,8,8,128]{0,3,2,1:T(8,128)} %broadcast_bitcast_fusion), kind=kLoop, calls=%fused_computation | loop fusion | flops 786432 | bytes 2097152 | tf_op jit(solution)/shard_map/mul | solution.py:109
  333.1 4.5 copy.422
  337.6 3.5 all-to-all-start.3
  341.1 11.7 %slice_bitcast_fusion.1 = (bf16[16,2,32,16,256]{4,3,2,1,0:T(8,128)(2,1)}, bf16[16,2,32,16,256]{4,3,2,1,0:T(8,128)(2,1)}) fusion(bf16[16,2,32,2,16,256]{5,4,3,2,1,0:T(8,128)(2,1)} %param.7), kind=kLoop, calls=%fused_computation.4 | loop fusion | bytes 33554432 | tf_op jit(solution)/shard_map/squeeze | solution.py:45
  353.0 3.1 copy.424
  356.1 4.8 fusion.197
  361.0 4.2 copy.499
  365.2 5.1 copy.500
  370.3 6.0 fusion.104
  376.4 6.1 %fusion.107 = f32[16,2,8,256]{3,2,1,0:T(8,128)S(1)} fusion(bf16[16,2,32,16,256]{4,3,2,1,0:T(8,128)(2,1)} %get-tuple-element.5, bf16[16,2,32,1,16,8]{2,5,4,1,0,3:T(8,128)(2,1)S(1)} %copy-done.7), kind=kOutput, calls=%fused_computation.85 | convolution fusion | flops 67108864 | bytes 8912896 | tf_op jit(solution)/shard_map/fijkq,fijkv->fviq/dot_general | solution.py:117
  385.0 2.6 fusion.116
  388.0 9.5 %fusion.2 = f32[16,2,8,32,16]{3,2,4,1,0:T(8,128)S(1)} fusion(bf16[16,2,32,16,256]{4,3,2,1,0:T(8,128)(2,1)} %get-tuple-element.6, bf16[16,1,8,2,256]{4,3,2,1,0:T(2,128)(2,1)S(1)} %get-tuple-element.15), kind=kOutput, calls=%fused_computation.7 | convolution fusion | flops 67108864 | bytes 9043968 | tf_op jit(solution)/shard_map/fijkq,fviq->fijkv/dot_general | solution.py:57
  397.4 9.1 %fusion = f32[16,2,8,32,16]{3,2,4,1,0:T(8,128)S(1)} fusion(bf16[16,2,32,16,256]{4,3,2,1,0:T(8,128)(2,1)} %get-tuple-element.6, bf16[16,1,8,2,256]{4,3,2,1,0:T(2,128)(2,1)S(1)} %get-tuple-element.16), kind=kOutput, calls=%fused_computation.5 | convolution fusion | flops 67108864 | bytes 9043968 | tf_op jit(solution)/shard_map/fijkq,fviq->fijkv/dot_general | solution.py:57
  406.5 6.9 %add_bitcast_fusion.1 = f32[16,2,32,1,128]{2,4,1,0,3:T(8,128)} fusion(f32[16,2,8,32,16]{3,2,4,1,0:T(8,128)S(1)} %fusion.2, bf16[16,2,32,16,256]{4,3,2,1,0:T(8,128)(2,1)S(1)} %bitcast.365, bf16[16,1,8,2,256]{4,3,2,1,0:T(2,128)(2,1)S(1)} %get-tuple-element.16), kind=kOutput, calls=%fused_computation.61 | convolution fusion | flops 67239936 | bytes 9568256 | tf_op jit(solution)/shard_map/fijkq,fviq->fijkv/dot_general | solution.py:57
  413.4 7.0 %subtract_bitcast_fusion.1 = f32[16,2,32,1,128]{2,4,1,0,3:T(8,128)} fusion(f32[16,2,8,32,16]{3,2,4,1,0:T(8,128)S(1)} %fusion, bf16[16,2,32,16,256]{4,3,2,1,0:T(8,128)(2,1)S(1)} %bitcast.365, bf16[16,1,8,2,256]{4,3,2,1,0:T(2,128)(2,1)S(1)} %get-tuple-element.15), kind=kOutput, calls=%fused_computation.60 | convolution fusion | flops 67239936 | bytes 9568256 | tf_op jit(solution)/shard_map/fijkq,fviq->fijkv/dot_general | solution.py:57
  422.7 3.0 copy.437
  428.0 4.8 all-to-all-start.4
  434.4 9.8 %all-to-all-done.4 = bf16[16,2,32,2,128]{4,0,3,1,2:T(8,128)(2,1)S(1)} async-done(((bf16[16,2,32,2,128]{4,0,3,1,2:T(8,128)(2,1)}), bf16[16,2,32,2,128]{4,0,3,1,2:T(8,128)(2,1)S(1)}, u32[]{:S(2)}, u32[]{:S(2)}) %all-to-all-start.4) | async-done | bytes 524320 | tf_op jit(solution)/shard_map/all_to_all | solution.py:67
  444.2 3.1 copy.441
  447.3 4.9 fusion.196
  452.1 5.7 copy.504
  457.9 5.5 fusion.74
  463.3 6.1 copy.503
  469.4 6.2 %fusion.77 = f32[16,8,8,256]{3,2,1,0:T(8,128)S(1)} fusion(bf16[16,8,8,1,16,256]{5,4,3,2,1,0:T(8,128)(2,1)} %get-tuple-element.8, bf16[16,8,8,1,16,8]{4,5,1,2,0,3:T(8,128)(2,1)} %copy.503), kind=kOutput, calls=%fused_computation.75 | convolution fusion | flops 67108864 | bytes 9699328 | tf_op jit(solution)/shard_map/fijkp,fijkv->fvjp/dot_general | solution.py:71
  475.6 5.7 fusion.95
  483.9 11.4 %copy.444 = f32[16,2,8,2048]{0,2,1,3:T(8,128)} copy(f32[16,2,8,2048]{3,2,1,0:T(8,128)S(1)} %fusion.28) | data formatting | bytes 4194304 | tf_op jit(solution)/shard_map/add | solution.py:124
  495.4 10.6 %reshape.103 = f32[8,1,65536]{2,1,0:T(1,128)S(1)} reshape(f32[2048,2,8,16]{3,2,1,0:T(8,128)} %bitcast.368) | data formatting | bytes 4194304
  506.0 33.1 %all_to_all.117 = f32[8,1,65536]{2,1,0:T(1,128)} all-to-all(f32[8,1,65536]{2,1,0:T(1,128)S(1)} %reshape.103), channel_id=1, replica_groups=mesh['freq'=8,'tile'=4] {'freq'}, dimensions={0} | all-to-all | bytes 4194304 | tf_op jit(solution)/shard_map/all_to_all | solution.py:84
  539.1 7.2 %reduce.1 = f32[8,65536]{1,0:T(8,128)S(1)} reduce(f32[8,1,65536]{2,1,0:T(1,128)} %all_to_all.117, f32[]{:T(128)} %broadcast.71), dimensions={1}, to_apply=%all_to_all.102.reduce_sub_computation | reduce | bytes 4194308 | tf_op jit(solution)/shard_map/all_to_all | solution.py:84
  546.3 11.3 %reshape.104 = f32[2048,2,8,16]{3,2,1,0:T(8,128)} reshape(f32[8,65536]{1,0:T(8,128)S(1)} %reduce.1) | data formatting | bytes 4194304
  557.6 9.9 %copy.446 = f32[8,16,2,8,256]{4,1,0,3,2:T(8,128)S(1)} copy(f32[8,16,2,8,256]{1,3,2,4,0:T(8,128)} %bitcast.369) | data formatting | bytes 4194304 | tf_op jit(solution)/shard_map/all_to_all | solution.py:84
  569.8 3.1 maximum_multiply_fusion.3
  577.8 29.0 %all_to_all.118 = f32[128,2,8,256]{3,2,1,0:T(8,128)S(1)} all-to-all(f32[128,2,8,256]{3,2,1,0:T(8,128)S(1)} %copy.451), channel_id=1, replica_groups=mesh['freq'=8,'tile'=4] {'freq'}, dimensions={0} | all-to-all | bytes 4194304 | tf_op jit(solution)/shard_map/all_to_all | solution.py:96
  (97 shorter events, 49.6 us)
Async XLA Ops:
  3.6 1.3 copy-start.4
  6.1 68.9 %copy-start.5 = (f32[16,2,32,128]{3,2,1,0:T(8,128)}, f32[16,2,32,128]{3,2,1,0:T(8,128)S(1)}, u32[]{:S(2)}) copy-start(f32[16,2,32,128]{3,2,1,0:T(8,128)S(1)} %copy.402) | copy-start | bytes 1572868
  77.4 21.0 %all-to-all-start = ((bf16[16,2,32,2,128]{4,0,3,1,2:T(8,128)(2,1)}), bf16[16,2,32,2,128]{4,0,3,1,2:T(8,128)(2,1)S(1)}, u32[]{:S(2)}, u32[]{:S(2)}) async-start(bf16[16,2,32,2,128]{4,0,3,1,2:T(8,128)(2,1)} %copy.403), calls=%async_computation | async-start | bytes 1048576 | tf_op jit(solution)/shard_map/all_to_all | solution.py:67
  118.1 11.8 %slice-start = ((s8[8388608]{0:T(1024)(128)(4,1)}), s8[4194304]{0:T(1024)(128)(4,1)S(1)}, s32[]{:S(2)}) async-start(s8[8388608]{0:T(1024)(128)(4,1)} %bitcast.354), calls=%async_computation.7 | async-start | bytes 8388608
  124.3 5.6 slice-start.1
  129.9 2.2 copy-start.2
  132.1 2.1 copy-start.9
  157.5 30.5 %all-to-all-start.1 = ((f32[8,1,65536]{2,1,0:T(1,128)}), f32[8,1,65536]{2,1,0:T(1,128)S(1)}, u32[]{:S(2)}, u32[]{:S(2)}) async-start(f32[8,1,65536]{2,1,0:T(1,128)} %reshape.101), calls=%async_computation.1 | async-start | bytes 4194304 | tf_op jit(solution)/shard_map/all_to_all | solution.py:84
  188.1 1.3 copy-start.1
  208.4 12.5 %copy-start.10 = (f32[8]{0:T(128)S(1)}, f32[8]{0:T(128)}, u32[]{:S(2)}) copy-start(f32[8]{0:T(128)} %param.13) | copy-start | bytes 100
  230.2 30.2 %all-to-all-start.2 = ((f32[128,2,8,256]{3,2,1,0:T(8,128)}), f32[128,2,8,256]{3,2,1,0:T(8,128)S(1)}, u32[]{:S(2)}, u32[]{:S(2)}) async-start(f32[128,2,8,256]{3,2,1,0:T(8,128)} %copy.417), calls=%async_computation.2 | async-start | bytes 4194304 | tf_op jit(solution)/shard_map/all_to_all | solution.py:96
  260.4 13.5 %slice-start.2 = ((s8[8388608]{0:T(1024)(128)(4,1)}), s8[4194304]{0:T(1024)(128)(4,1)S(1)}, s32[]{:S(2)}) async-start(s8[8388608]{0:T(1024)(128)(4,1)} %bitcast.356), calls=%async_computation.9 | async-start | bytes 8388608
  260.5 13.4 %slice-start.3 = ((s8[8388608]{0:T(1024)(128)(4,1)}), s8[4194304]{0:T(1024)(128)(4,1)S(1)}, s32[]{:S(2)}) async-start(s8[8388608]{0:T(1024)(128)(4,1)} %bitcast.356), calls=%async_computation.10 | async-start | bytes 8388608
  260.5 25.1 %slice-start.8 = ((s8[8388608]{0:T(1024)(128)(4,1)}), s8[4194304]{0:T(1024)(128)(4,1)S(1)}, s32[]{:S(2)}) async-start(s8[8388608]{0:T(1024)(128)(4,1)} %bitcast.362), calls=%async_computation.15 | async-start | bytes 8388608
  273.9 11.8 %slice-start.9 = ((s8[8388608]{0:T(1024)(128)(4,1)}), s8[4194304]{0:T(1024)(128)(4,1)S(1)}, s32[]{:S(2)}) async-start(s8[8388608]{0:T(1024)(128)(4,1)} %bitcast.362), calls=%async_computation.16 | async-start | bytes 8388608
  337.6 15.4 %all-to-all-start.3 = ((bf16[16,8,8,2,128]{4,2,3,0,1:T(8,128)(2,1)}), bf16[16,8,8,2,128]{4,2,3,0,1:T(8,128)(2,1)S(1)}, u32[]{:S(2)}, u32[]{:S(2)}) async-start(bf16[16,8,8,2,128]{4,2,3,0,1:T(8,128)(2,1)} %copy.422), calls=%async_computation.3 | async-start | bytes 1048576 | tf_op jit(solution)/shard_map/all_to_all | solution.py:113
  370.3 6.0 copy-start.7
  370.3 12.1 %slice-start.6 = ((s8[8388608]{0:T(1024)(128)(4,1)}), s8[4194304]{0:T(1024)(128)(4,1)S(1)}, s32[]{:S(2)}) async-start(s8[8388608]{0:T(1024)(128)(4,1)} %bitcast.360), calls=%async_computation.13 | async-start | bytes 8388608
  376.4 6.1 %slice-start.7 = ((s8[8388608]{0:T(1024)(128)(4,1)}), s8[4194304]{0:T(1024)(128)(4,1)S(1)}, s32[]{:S(2)}) async-start(s8[8388608]{0:T(1024)(128)(4,1)} %bitcast.360), calls=%async_computation.14 | async-start | bytes 8388608
  385.0 2.6 copy-start.8
  388.0 18.5 %slice-start.10 = ((s8[8388608]{0:T(1024)(128)(4,1)}), s8[4194304]{0:T(1024)(128)(4,1)S(1)}, s32[]{:S(2)}) async-start(s8[8388608]{0:T(1024)(128)(4,1)} %bitcast.364), calls=%async_computation.17 | async-start | bytes 8388608
  397.4 9.1 %slice-start.11 = ((s8[8388608]{0:T(1024)(128)(4,1)}), s8[4194304]{0:T(1024)(128)(4,1)S(1)}, s32[]{:S(2)}) async-start(s8[8388608]{0:T(1024)(128)(4,1)} %bitcast.364), calls=%async_computation.18 | async-start | bytes 8388608
  420.4 5.2 copy-start.6
  428.0 16.2 %all-to-all-start.4 = ((bf16[16,2,32,2,128]{4,0,3,1,2:T(8,128)(2,1)}), bf16[16,2,32,2,128]{4,0,3,1,2:T(8,128)(2,1)S(1)}, u32[]{:S(2)}, u32[]{:S(2)}) async-start(bf16[16,2,32,2,128]{4,0,3,1,2:T(8,128)(2,1)} %copy.439), calls=%async_computation.4 | async-start | bytes 1048576 | tf_op jit(solution)/shard_map/all_to_all | solution.py:67
  469.4 6.2 %copy-start.3 = (bf16[16,8,8,1,16,8]{4,5,1,2,0,3:T(8,128)(2,1)S(1)}, bf16[16,8,8,1,16,8]{4,5,1,2,0,3:T(8,128)(2,1)}, u32[]{:S(2)}) copy-start(bf16[16,8,8,1,16,8]{4,5,1,2,0,3:T(8,128)(2,1)} %copy.503) | copy-start | bytes 786436
  469.4 11.9 %slice-start.4 = ((s8[8388608]{0:T(1024)(128)(4,1)}), s8[4194304]{0:T(1024)(128)(4,1)S(1)}, s32[]{:S(2)}) async-start(s8[8388608]{0:T(1024)(128)(4,1)} %bitcast.358), calls=%async_computation.11 | async-start | bytes 8388608
  475.6 5.7 slice-start.5
  481.3 2.2 copy-start
where the time goes:
time: 619 us; the launch traced here: 609 us
  matrix products  218 us (35%)
  local copies, waits for them, and re-layouts  216 us (35%)
  blocking collectives  62.1 us (10%)
  waiting for transfers between devices  61.9 us (10%)
  other arithmetic  27 us (4%)
  starting transfers between devices  22.5 us (4%)
    dot_general x8, matrix products, contract_left(): jnp.einsum('fijkq,fviq->fijkv', matrix, vectors, preferred_element_type=j...  93.6 us
    unnamed x57, local copies, waits for them, and re-layouts  81.3 us
    dot_general x4, matrix products, project(): jnp.einsum('fijkp,fvjp->fijkv', matrix, vectors, preferred_element_type=j...  53.7 us
    dot_general x8, matrix products, spread(): jnp.einsum('fijkp,fijkv->fvjp', matrix, vectors, preferred_element_type=j...  35.6 us
    all_to_all x1, blocking collectives, to_time(): lax.all_to_all(wavefield, 'freq', split_axis=3, concat_axis=0, tiled=True)  33.1 us
    all_to_all x1, blocking collectives, to_freq(): lax.all_to_all(jnp.stack([real_part, imag_part], 1), 'freq', split_axis=0...  29 us
    all_to_all x1, waiting for transfers between devices, to_time(): lax.all_to_all(wavefield, 'freq', split_axis=3, concat_axis=0, tiled=True)  26.6 us
    all_to_all x1, waiting for transfers between devices, to_freq(): lax.all_to_all(jnp.stack([real_part, imag_part], 1), 'freq', split_axis=0...  22.8 us
  transfers between devices with their start and end apart: 5, of which 5 were waited for; matrix products, arithmetic and copies ran while one was open for 5% of the time, Pallas kernels for 0%

commit v1 on v0

--- a/solution.py
+++ b/solution.py
@@ -1,8 +1,12 @@
+import functools
 import math
 
 import jax
 import jax.numpy as jnp
+import numpy as np
 from jax import lax
+from jax.experimental import pallas as pl
+from jax.experimental.pallas import tpu as pltpu
 from jax.sharding import PartitionSpec as P
 
 F = 128
@@ -24,7 +28,7 @@
     return (tile_scales[:, 0] * tile_scales[:, 1])[..., None] * live_slots
 
 
-def per_device(
+def per_device_plain(
     left_factor, right_factor, tile_ranks, tile_scales, recorded, step_sizes, thresholds
 ):
     freqs_here = left_factor.shape[0]
@@ -134,9 +138,341 @@
     )
 
 
+def swap_parts(values, first_part, half):
+    pieces = []
+    for start in range(0, values.shape[1], 128):
+        piece = values[:, start : start + 128]
+        pieces.append(
+            jnp.where(
+                first_part, pltpu.roll(piece, 128 - half, 1), pltpu.roll(piece, half, 1)
+            )
+        )
+    return jnp.concatenate(pieces, 1)
+
+
+def lane_ids(rows, lanes):
+    return lax.broadcasted_iota(jnp.int32, (rows, lanes), 1)
+
+
+def adjoint_rows(product, half):
+    virtual = product.shape[0] // 2
+    lanes = product.shape[1]
+    sign = jnp.where(lane_ids(virtual, lanes) // half % 2 == 0, 1.0, -1.0)
+    first_part = lane_ids(virtual, 128) // half % 2 == 0
+    return product[:virtual] * sign + swap_parts(product[virtual:], first_part, half)
+
+
+def forward_rows(coefs, half):
+    rows, lanes = coefs.shape
+    sign = jnp.where(lane_ids(rows, lanes) // half % 2 == 0, 1.0, -1.0)
+    first_part = lane_ids(rows, 128) // half % 2 == 0
+    return coefs * sign, swap_parts(coefs, first_part, half)
+
+
+def nt_dot(a, b):
+    return lax.dot_general(a, b, (((1,), (1,)), ((), ())), preferred_element_type=jnp.float32)
+
+
+def nn_dot(a, b):
+    return jnp.dot(a, b, preferred_element_type=jnp.float32)
+
+
+def dual_of(left_rows, field, weight, half):
+    return adjoint_rows(nt_dot(field.astype(jnp.bfloat16), left_rows), half) * weight
+
+
+def store_duals(out_ref, at, duals, peers):
+    together = jnp.concatenate(duals, 0)
+    width = together.shape[1] // peers
+    for peer in range(peers):
+        out_ref[peer, at] = together[:, peer * width : (peer + 1) * width].astype(jnp.bfloat16)
+
+
+def dual_kernel(left_ref, recorded_ref, weight_ref, out_ref):
+    freqs, rows, cols, _, rank, width = left_ref.shape
+    peers = out_ref.shape[0]
+    for at in range(freqs):
+        duals = []
+        for row in range(rows):
+            left_rows = left_ref[at, row].reshape(cols * 2 * rank, width)
+            part = recorded_ref[at, :, :, row * width : (row + 1) * width]
+            field = part.reshape(-1, width)
+            duals.append(dual_of(left_rows, field, weight_ref[at, row : row + 1], rank))
+        store_duals(out_ref, at, duals, peers)
+
+
+def image_kernel(left_ref, coefs_ref, recorded_ref, weight_ref, out_ref):
+    freqs, rows, cols, _, rank, width = left_ref.shape
+    peers = coefs_ref.shape[0]
+    share = cols // peers * 2 * rank
+    virtual = recorded_ref.shape[2]
+    for at in range(freqs):
+        forms = [
+            forward_rows(coefs_ref[peer, at].astype(jnp.float32), rank) for peer in range(peers)
+        ]
+        duals = []
+        for row in range(rows):
+            left_rows = left_ref[at, row].reshape(cols * 2 * rank, width)
+            own = slice(row * virtual, (row + 1) * virtual)
+            image = 0.0
+            for peer, (real_form, imag_form) in enumerate(forms):
+                both = jnp.concatenate([real_form[own], imag_form[own]], 0).astype(jnp.bfloat16)
+                image += nn_dot(both, left_rows[peer * share : (peer + 1) * share])
+            part = recorded_ref[at, :, :, row * width : (row + 1) * width]
+            field = part.reshape(-1, width) - image
+            duals.append(dual_of(left_rows, field, weight_ref[at, row : row + 1], rank))
+        store_duals(out_ref, at, duals, peers)
+
+
+def spread_kernel(steps_ref, right_ref, duals_ref, out_ref):
+    freqs, rows, cols, _, rank, width = right_ref.shape
+    peers, _, both, share = duals_ref.shape
+    rows_each = rows // peers
+    virtual = both // rows_each
+    group = 2 * rank
+    owner = lane_ids(2 * virtual, share) // group
+    for at in range(freqs):
+        wide = []
+        for peer in range(peers):
+            real_form, imag_form = forward_rows(duals_ref[peer, at].astype(jnp.float32), rank)
+            for row in range(rows_each):
+                own = slice(row * virtual, (row + 1) * virtual)
+                rows_both = jnp.concatenate([real_form[own], imag_form[own]], 0)
+                wide.append(
+                    jnp.concatenate(
+                        [jnp.where(owner == col, rows_both, 0.0) for col in range(cols)], 0
+                    ).astype(jnp.bfloat16)
+                )
+        total = 0.0
+        for row in range(rows):
+            total += nn_dot(wide[row], right_ref[at, row].reshape(cols * group, width))
+        step = steps_ref[pl.program_id(0) * freqs + at]
+        out_ref[:, at] = (total * step).astype(jnp.bfloat16).reshape(cols, 2 * virtual, width)
+
+
+def project_kernel(right_ref, field_ref, weight_ref, out_ref):
+    freqs, rows, cols, _, rank, width = right_ref.shape
+    peers, _, both, share = out_ref.shape
+    rows_each = rows // peers
+    virtual = both // rows_each
+    group = 2 * rank
+    owner = lane_ids(2 * virtual, 128) // group
+    per_piece = 128 // group
+    for at in range(freqs):
+        field = field_ref[:, at].reshape(cols * 2 * virtual, width)
+        for peer in range(peers):
+            coefs = []
+            for row in range(peer * rows_each, (peer + 1) * rows_each):
+                product = nt_dot(field, right_ref[at, row].reshape(cols * group, width))
+                pieces = []
+                for start in range(0, share, 128):
+                    piece = 0.0
+                    for step in range(per_piece):
+                        col = start // group + step
+                        rows_of = product[
+                            col * 2 * virtual : (col + 1) * 2 * virtual, start : start + 128
+                        ]
+                        piece = rows_of if step == 0 else jnp.where(owner == step, rows_of, piece)
+                    pieces.append(piece)
+                picked = jnp.concatenate(pieces, 1)
+                coefs.append(adjoint_rows(picked, rank) * weight_ref[at, row : row + 1])
+            out_ref[peer, at] = jnp.concatenate(coefs, 0).astype(jnp.bfloat16)
+
+
+def split_two(values):
+    high = values.astype(jnp.bfloat16)
+    return high, (values - high.astype(jnp.float32)).astype(jnp.bfloat16)
+
+
+def shrink_kernel(second, *refs):
+    if second:
+        (levels_ref, to_high, to_low, back_high, back_low, field_ref, kept_ref, out_ref,
+         wide, packed) = refs
+    else:
+        (levels_ref, to_high, to_low, back_high, back_low, field_ref, out_ref, kept_ref,
+         wide, packed) = refs
+    virtual = levels_ref.shape[0]
+    peers, freqs, rows, width = field_ref.shape
+    times = to_high.shape[0]
+    lines = peers * freqs * 2
+    halves = [slice(at, at + 128) for at in range(0, width, 128)]
+    for half, lanes in enumerate(halves):
+        wide[half] = (
+            field_ref[:, :, :, lanes].astype(jnp.float32).reshape(lines * virtual, 128)
+        )
+    if not second:
+        odd = lax.broadcasted_iota(jnp.int32, (times, width), 0) % 2
+        turn = jnp.where(odd == 0, 1.0, -1.0)
+    for source in range(virtual):
+        own = pl.ds(source, lines, stride=virtual)
+        spectrum = jnp.concatenate(
+            [wide[half, own, :] for half in range(len(halves))], 1
+        ).astype(jnp.bfloat16)
+        signal = nn_dot(to_high[...], spectrum) + nn_dot(to_low[...], spectrum)
+        if second:
+            signal += kept_ref[source]
+        level = levels_ref[source]
+        shrunk = signal - jnp.clip(signal, -level, level)
+        if not second:
+            mean = jnp.sum(shrunk * turn, 0, keepdims=True) * (1.0 / times)
+            kept_ref[source] = shrunk - turn * mean
+        high, low = split_two(shrunk)
+        freq = nn_dot(back_high[...], high) + nn_dot(back_low[...], high) + nn_dot(
+            back_high[...], low
+        )
+        for half, lanes in enumerate(halves):
+            packed[half, own, :] = freq[:, lanes]
+    for half, lanes in enumerate(halves):
+        out_ref[:, :, :, lanes] = (
+            packed[half].astype(jnp.bfloat16).reshape(peers, freqs, rows, 128)
+        )
+
+
+def table_parts():
+    times = 2 * F
+    freq = np.arange(F)[:, None]
+    angles = (freq * np.arange(times)[None, :] % times) * (2.0 * math.pi / times)
+    scaling = np.where(freq == 0, math.sqrt(1.0 / times), math.sqrt(2.0 / times))
+    table = np.stack([scaling * np.cos(angles), -scaling * np.sin(angles)], 1)
+    table = table.reshape(2 * F, times).astype(np.float32)
+    high = table.astype(jnp.bfloat16)
+    low = (table - high.astype(np.float32)).astype(jnp.bfloat16)
+    return tuple(jnp.asarray(part) for part in (high.T, low.T, high, low))
+
+
+def vmem():
+    return pl.BlockSpec(memory_space=pltpu.VMEM)
+
+
+def smem():
+    return pl.BlockSpec(memory_space=pltpu.SMEM)
+
+
+PARAMS = pltpu.CompilerParams(vmem_limit_bytes=48 << 20, dimension_semantics=("arbitrary",))
+
+
+def per_device(
+    left_factor, right_factor, tile_ranks, tile_scales, recorded, step_sizes, thresholds
+):
+    freqs, rows_here, col_tiles, _, rank, width = left_factor.shape
+    row_tiles, cols_here = right_factor.shape[1:3]
+    virtual = recorded.shape[2]
+    tile_size = col_tiles // cols_here
+    share = cols_here * 2 * rank
+    lines = rows_here * virtual
+    tile_pos = lax.axis_index("tile")
+    block = 2 if freqs % 2 == 0 else 1
+    grid = (freqs // block,)
+
+    weights = slot_weights(tile_ranks, tile_scales, rank)
+    weights = jnp.broadcast_to(
+        weights[:, :, :, None, :], (freqs, row_tiles, col_tiles, 2, rank)
+    ).reshape(freqs, row_tiles, col_tiles * 2 * rank)
+    weights_left = lax.dynamic_slice_in_dim(weights, tile_pos * rows_here, rows_here, 1)
+    weights_right = lax.dynamic_slice_in_dim(weights, tile_pos * share, share, 2)
+
+    def by_freq(array):
+        rest = array.shape[1:]
+        return pl.BlockSpec((block,) + rest, lambda f: (f,) + (0,) * len(rest))
+
+    def by_second(shape):
+        return pl.BlockSpec((shape[0], block) + shape[2:], lambda f: (0, f, 0, 0))
+
+    coef_shape = (tile_size, freqs, lines, share)
+    field_shape = (cols_here, freqs, 2 * virtual, width)
+    coef_type = jax.ShapeDtypeStruct(coef_shape, jnp.bfloat16)
+    field_type = jax.ShapeDtypeStruct(field_shape, jnp.bfloat16)
+
+    def spread(duals):
+        return pl.pallas_call(
+            spread_kernel,
+            out_shape=field_type,
+            grid=grid,
+            in_specs=[smem(), by_freq(right_factor), by_second(coef_shape)],
+            out_specs=by_second(field_shape),
+            compiler_params=PARAMS,
+        )(step_sizes, right_factor, duals)
+
+    def over_tile(array):
+        return lax.all_to_all(array, "tile", split_axis=0, concat_axis=0, tiled=True)
+
+    def over_freq(array):
+        return lax.all_to_all(array, "freq", split_axis=0, concat_axis=0, tiled=True)
+
+    times = 2 * F
+    kept_type = jax.ShapeDtypeStruct((virtual, times, width), jnp.float32)
+    tables = table_parts()
+    scratch = [pltpu.VMEM((width // 128, times * virtual, 128), jnp.float32)] * 2
+
+    duals = pl.pallas_call(
+        dual_kernel,
+        out_shape=coef_type,
+        grid=grid,
+        in_specs=[by_freq(left_factor), by_freq(recorded), by_freq(weights_left)],
+        out_specs=by_second(coef_shape),
+        compiler_params=PARAMS,
+    )(left_factor, recorded, weights_left)
+    gradient = over_freq(spread(over_tile(duals)))
+    first, kept = pl.pallas_call(
+        functools.partial(shrink_kernel, False),
+        out_shape=[field_type, kept_type],
+        in_specs=[smem()] + [vmem()] * 5,
+        out_specs=[vmem(), vmem()],
+        scratch_shapes=scratch,
+        compiler_params=pltpu.CompilerParams(vmem_limit_bytes=48 << 20),
+    )(thresholds, *tables, gradient)
+    coefs = pl.pallas_call(
+        project_kernel,
+        out_shape=coef_type,
+        grid=grid,
+        in_specs=[by_freq(right_factor), by_second(field_shape), by_freq(weights_right)],
+        out_specs=by_second(coef_shape),
+        compiler_params=PARAMS,
+    )(right_factor, over_freq(first), weights_right)
+    duals = pl.pallas_call(
+        image_kernel,
+        out_shape=coef_type,
+        grid=grid,
+        in_specs=[
+            by_freq(left_factor),
+            by_second(coef_shape),
+            by_freq(recorded),
+            by_freq(weights_left),
+        ],
+        out_specs=by_second(coef_shape),
+        compiler_params=PARAMS,
+    )(left_factor, over_tile(coefs), recorded, weights_left)
+    gradient = over_freq(spread(over_tile(duals)))
+    estimate = pl.pallas_call(
+        functools.partial(shrink_kernel, True),
+        out_shape=field_type,
+        in_specs=[smem()] + [vmem()] * 6,
+        out_specs=vmem(),
+        scratch_shapes=scratch,
+        compiler_params=pltpu.CompilerParams(vmem_limit_bytes=48 << 20),
+    )(thresholds, *tables, gradient, kept)
+    arrived = over_freq(estimate).astype(jnp.float32)
+    return arrived.transpose(1, 2, 0, 3).reshape(freqs, 2, virtual, cols_here * width)
+
+
+def either(*arrays):
+    left_factor, right_factor = arrays[:2]
+    cols_here = right_factor.shape[2]
+    rank, width = left_factor.shape[4:]
+    aligned = (
+        cols_here == lax.axis_size("freq")
+        and width % 128 == 0
+        and 128 % (2 * rank) == 0
+        and (cols_here * 2 * rank) % 128 == 0
+        and arrays[4].shape[2] == 8
+        and left_factor.shape[0] * lax.axis_size("freq") == F
+    )
+    return (per_device if aligned else per_device_plain)(*arrays)
+
+
 def solution(mesh):
     return jax.shard_map(
-        per_device,
+        either,
         mesh=mesh,
         in_specs=(
             P("freq", "tile", None, None, None, None),

time: 619 us -> 210 us (0.34); the launches traced: 609 us -> 209 us
  matrix products: 218 us -> 0 us
  local copies, waits for them, and re-layouts: 216 us -> 16.2 us
  Pallas kernels: 0 us -> 61.9 us
  waiting for transfers between devices: 61.9 us -> 15.3 us
  blocking collectives: 62.1 us -> 108 us
  other arithmetic: 27 us -> 3.13 us
  starting transfers between devices: 22.5 us -> 3.56 us
    dot_general x32 -> x0, matrix products: 218 us -> none  [the longest x8 93.6 us: contract_left(): jnp.einsum('fijkq,fviq->fijkv', matrix, vectors, preferred_element_type=j...]
    unnamed x57 -> x18, local copies, waits for them, and re-layouts: 81.3 us -> 1.37 us
    pallas_call x0 -> x7, Pallas kernels: none -> 61.9 us  [the longest x2 19 us: spread(): pl.pallas_call(spread_kernel, out_shape=field_type, grid=grid, in_specs=[...]
    all_to_all x5 -> x1, waiting for transfers between devices: 61.9 us -> 15.3 us  [over_freq(): lax.all_to_all(array, 'freq', split_axis=0, concat_axis=0, tiled=True)]
    all_to_all x2 -> x6, blocking collectives: 62.1 us -> 108 us  [the longest x3 57.6 us: over_freq(): lax.all_to_all(array, 'freq', split_axis=0, concat_axis=0, tiled=True)]
    all_to_all x9 -> x0, local copies, waits for them, and re-layouts: 33.3 us -> none  [the longest x3 20.7 us: to_time(): lax.all_to_all(wavefield, 'freq', split_axis=3, concat_axis=0, tiled=True)]
    slice x6 -> x0, local copies, waits for them, and re-layouts: 26.8 us -> none  [the longest x1 11.9 us: per_device(): right_real = right_factor[:, :, :, 0]]
    add x3 -> x0, local copies, waits for them, and re-layouts: 20.4 us -> none  [the longest x1 11.4 us: per_device(): first + scaled * gradient(recorded - jnp.stack([image_real, image_imag],...]
  transfers between devices with their start and end apart: 5 -> 1, of which waited for: 5 -> 1; matrix products, arithmetic and copies ran while one was open for 5% -> 0% of each run, Pallas kernels for 0% -> 0%
where the time goes in v1:
time: 210 us; the launch traced here: 209 us
  blocking collectives  108 us (51%)
  Pallas kernels  61.9 us (29%)
  local copies, waits for them, and re-layouts  16.2 us (8%)
  waiting for transfers between devices  15.3 us (7%)
  starting transfers between devices  3.56 us (2%)
  other arithmetic  3.13 us (1%)
    all_to_all x3, blocking collectives, over_freq(): lax.all_to_all(array, 'freq', split_axis=0, concat_axis=0, tiled=True)  57.6 us
    all_to_all x3, blocking collectives, over_tile(): lax.all_to_all(array, 'tile', split_axis=0, concat_axis=0, tiled=True)  50.8 us
    pallas_call x2, Pallas kernels, spread(): pl.pallas_call(spread_kernel, out_shape=field_type, grid=grid, in_specs=[...  19 us
    all_to_all x1, waiting for transfers between devices, over_freq(): lax.all_to_all(array, 'freq', split_axis=0, concat_axis=0, tiled=True)  15.3 us
    pallas_call x1, Pallas kernels, per_device(): pl.pallas_call(image_kernel, out_shape=coef_type, grid=grid, in_specs=[by...  13.4 us
    pallas_call x1, Pallas kernels, per_device(): pl.pallas_call(project_kernel, out_shape=coef_type, grid=grid, in_specs=[...  11.3 us
    pallas_call x1, Pallas kernels, per_device(): pl.pallas_call(dual_kernel, out_shape=coef_type, grid=grid, in_specs=[by_...  10.5 us
    reshape x1, local copies, waits for them, and re-layouts, per_device(): weights = jnp.broadcast_to(weights[:, :, :, None, :], (freqs, row_tiles,...  7.95 us
  transfers between devices with their start and end apart: 1, of which 1 were waited for; matrix products, arithmetic and copies ran while one was open for 0% of the time, Pallas kernels for 0%

profile of v1, /device:TPU:0, one launch (start us, length us, event | category | flops | bytes accessed | tf_op | source)
XLA Modules:
  0.0 208.6 jit_solution(15052271686815453792)
XLA Ops:
  0.0 0.9 multiply_bitcast_fusion
  0.9 2.0 fusion
  2.9 3.6 %broadcast_in_dim.2 = f32[16,8,32,2,16]{4,3,2,1,0:T(2,128)} broadcast(f32[16,8,32,16]{3,2,1,0:T(8,128)S(1)} %fusion), dimensions={0,1,2,4} | broadcast | bytes 786432 | tf_op jit(solution)/shard_map/broadcast_in_dim | solution.py:368
  6.5 0.0 copy-start
  6.5 7.9 %reshape.24 = f32[16,8,1024]{2,1,0:T(8,128)S(1)} reshape(f32[16,8,32,2,16]{4,3,2,1,0:T(2,128)} %broadcast_in_dim.2) | data formatting | bytes 1048576 | tf_op jit(solution)/shard_map/reshape | solution.py:370
  14.5 0.1 constant_dynamic-slice_fusion.1.weight_ref
  14.5 0.0 copy-done
  14.5 0.0 copy-start.7
  14.6 10.5 %shard_map.109 = bf16[4,16,16,256]{3,2,1,0:T(8,128)(2,1)S(1)} custom-call(bf16[16,2,32,2,16,256]{5,4,3,2,1,0:T(8,128)(2,1)} %left_ref.3, f32[16,2,8,512]{3,2,1,0:T(8,128)S(1)} %copy-done, f32[16,2,1024]{2,1,0:T(2,128)S(1)} %constant_dynamic-slice_fusion.1.weight_ref), custom_call_target="tpu_custom_call" | custom-call | tf_op jit(solution)/shard_map/pallas_call | solution.py:407
  25.1 20.6 %all_to_all.35.duals_ref = bf16[4,16,16,256]{3,2,1,0:T(8,128)(2,1)S(1)} all-to-all(bf16[4,16,16,256]{3,2,1,0:T(8,128)(2,1)S(1)} %shard_map.109), channel_id=1, replica_groups=mesh['freq'=8,'tile'=4] {'tile'}, dimensions={0} | all-to-all | bytes 1048576 | tf_op jit(solution)/shard_map/all_to_all | solution.py:397
  45.7 0.0 copy-done.7
  45.7 9.5 %shard_map.110 = bf16[8,16,16,256]{3,2,1,0:T(8,128)(2,1)S(1)} custom-call(f32[16]{0:T(128)S(1)} %copy-done.7, bf16[16,8,8,2,16,256]{5,4,3,2,1,0:T(8,128)(2,1)} %right_ref.5, bf16[4,16,16,256]{3,2,1,0:T(8,128)(2,1)S(1)} %all_to_all.35.duals_ref), custom_call_target="tpu_custom_call" | custom-call | tf_op jit(solution)/shard_map/pallas_call | solution.py:387
  55.3 0.0 copy-start.3
  55.3 0.0 copy-start.4
  55.3 0.0 copy-start.5
  55.3 0.0 copy-start.6
  55.3 0.0 copy-start.8
  55.3 19.0 %all_to_all.36.refs_5_ = bf16[8,16,16,256]{3,2,1,0:T(8,128)(2,1)S(1)} all-to-all(bf16[8,16,16,256]{3,2,1,0:T(8,128)(2,1)S(1)} %shard_map.110), channel_id=1, replica_groups=mesh['freq'=8,'tile'=4] {'freq'}, dimensions={0} | all-to-all | bytes 2097152 | tf_op jit(solution)/shard_map/all_to_all | solution.py:400
  74.3 0.0 copy-done.3
  74.3 0.0 copy-done.4
  74.3 0.0 copy-done.5
  74.3 0.0 copy-done.6
  74.3 0.0 copy-done.8
  74.3 4.3 %shard_map.111 = (bf16[8,16,16,256]{3,2,1,0:T(8,128)(2,1)}, f32[8,256,256]{2,1,0:T(8,128)S(1)}) custom-call(f32[8]{0:T(128)S(1)} %copy-done.8, bf16[256,256]{1,0:T(8,128)(2,1)S(1)} %copy-done.3, bf16[256,256]{1,0:T(8,128)(2,1)S(1)} %copy-done.4, bf16[256,256]{1,0:T(8,128)(2,1)S(1)} %copy-done.5, bf16[256,256]{1,0:T(8,128)(2,1)S(1)} %copy-done.6, ...), custom_call_target="tpu_custom_call" | custom-call | tf_op jit(solution)/shard_map/pallas_call | solution.py:416
  78.7 0.0 copy-start.1
  78.7 1.3 copy-done.1
  80.0 3.6 %all-to-all-start.2 = ((bf16[8,16,16,256]{3,2,1,0:T(8,128)(2,1)}), bf16[8,16,16,256]{3,2,1,0:T(8,128)(2,1)S(1)}, u32[]{:S(2)}, u32[]{:S(2)}) async-start(bf16[8,16,16,256]{3,2,1,0:T(8,128)(2,1)} %get-tuple-element.7), calls=%async_computation.2 | async-start | bytes 2097152 | tf_op jit(solution)/shard_map/all_to_all | solution.py:400
  83.6 15.3 %all-to-all-done.2.field_ref = bf16[8,16,16,256]{3,2,1,0:T(8,128)(2,1)S(1)} async-done(((bf16[8,16,16,256]{3,2,1,0:T(8,128)(2,1)}), bf16[8,16,16,256]{3,2,1,0:T(8,128)(2,1)S(1)}, u32[]{:S(2)}, u32[]{:S(2)}) %all-to-all-start.2) | async-done | bytes 1048608 | tf_op jit(solution)/shard_map/all_to_all | solution.py:400
  98.9 11.3 %shard_map.112 = bf16[4,16,16,256]{3,2,1,0:T(8,128)(2,1)S(1)} custom-call(bf16[16,8,8,2,16,256]{5,4,3,2,1,0:T(8,128)(2,1)} %right_ref.5, bf16[8,16,16,256]{3,2,1,0:T(8,128)(2,1)S(1)} %all-to-all-done.2.field_ref, f32[16,8,256]{2,1,0:T(8,128)S(1)} %constant_dynamic-slice_fusion.weight_ref), custom_call_target="tpu_custom_call" | custom-call | tf_op jit(solution)/shard_map/pallas_call | solution.py:424
  110.2 14.3 %all_to_all.37.coefs_ref = bf16[4,16,16,256]{3,2,1,0:T(8,128)(2,1)S(1)} all-to-all(bf16[4,16,16,256]{3,2,1,0:T(8,128)(2,1)S(1)} %shard_map.112), channel_id=1, replica_groups=mesh['freq'=8,'tile'=4] {'tile'}, dimensions={0} | all-to-all | bytes 1048576 | tf_op jit(solution)/shard_map/all_to_all | solution.py:397
  124.5 13.4 %shard_map.113 = bf16[4,16,16,256]{3,2,1,0:T(8,128)(2,1)S(1)} custom-call(bf16[16,2,32,2,16,256]{5,4,3,2,1,0:T(8,128)(2,1)} %left_ref.3, bf16[4,16,16,256]{3,2,1,0:T(8,128)(2,1)S(1)} %all_to_all.37.coefs_ref, f32[16,2,8,512]{3,2,1,0:T(8,128)S(1)} %copy-done, f32[16,2,1024]{2,1,0:T(2,128)S(1)} %constant_dynamic-slice_fusion.1.weight_ref), custom_call_target="tpu_custom_call" | custom-call | tf_op jit(solution)/shard_map/pallas_call | solution.py:432
  137.9 15.9 %all_to_all.38.duals_ref = bf16[4,16,16,256]{3,2,1,0:T(8,128)(2,1)S(1)} all-to-all(bf16[4,16,16,256]{3,2,1,0:T(8,128)(2,1)S(1)} %shard_map.113), channel_id=1, replica_groups=mesh['freq'=8,'tile'=4] {'tile'}, dimensions={0} | all-to-all | bytes 1048576 | tf_op jit(solution)/shard_map/all_to_all | solution.py:397
  153.8 9.5 %shard_map.114 = bf16[8,16,16,256]{3,2,1,0:T(8,128)(2,1)S(1)} custom-call(f32[16]{0:T(128)S(1)} %copy-done.7, bf16[16,8,8,2,16,256]{5,4,3,2,1,0:T(8,128)(2,1)} %right_ref.5, bf16[4,16,16,256]{3,2,1,0:T(8,128)(2,1)S(1)} %all_to_all.38.duals_ref), custom_call_target="tpu_custom_call" | custom-call | tf_op jit(solution)/shard_map/pallas_call | solution.py:387
  163.3 0.0 copy-start.2
  163.3 20.9 %all_to_all.39.refs_5_ = bf16[8,16,16,256]{3,2,1,0:T(8,128)(2,1)S(1)} all-to-all(bf16[8,16,16,256]{3,2,1,0:T(8,128)(2,1)S(1)} %shard_map.114), channel_id=1, replica_groups=mesh['freq'=8,'tile'=4] {'freq'}, dimensions={0} | all-to-all | bytes 2097152 | tf_op jit(solution)/shard_map/all_to_all | solution.py:400
  184.2 0.0 copy-done.2
  184.2 3.3 %shard_map.115 = bf16[8,16,16,256]{3,2,1,0:T(8,128)(2,1)S(1)} custom-call(f32[8]{0:T(128)S(1)} %copy-done.8, bf16[256,256]{1,0:T(8,128)(2,1)S(1)} %copy-done.3, bf16[256,256]{1,0:T(8,128)(2,1)S(1)} %copy-done.4, bf16[256,256]{1,0:T(8,128)(2,1)S(1)} %copy-done.5, bf16[256,256]{1,0:T(8,128)(2,1)S(1)} %copy-done.6, ...), custom_call_target="tpu_custom_call" | custom-call | tf_op jit(solution)/shard_map/pallas_call | solution.py:446
  187.4 17.8 %all_to_all.40 = bf16[8,16,16,256]{3,2,1,0:T(8,128)(2,1)S(1)} all-to-all(bf16[8,16,16,256]{3,2,1,0:T(8,128)(2,1)S(1)} %shard_map.115), channel_id=1, replica_groups=mesh['freq'=8,'tile'=4] {'freq'}, dimensions={0} | all-to-all | bytes 2097152 | tf_op jit(solution)/shard_map/all_to_all | solution.py:400
  205.2 0.3 convert_bitcast_fusion
  205.5 1.6 copy.12
  207.1 1.5 reshape.28
  (1 shorter events, 0.0 us)
Async XLA Ops:
  6.5 8.0 %copy-start = (f32[16,2,8,512]{3,2,1,0:T(8,128)S(1)}, f32[16,2,8,512]{3,2,1,0:T(8,128)}, u32[]{:S(2)}) copy-start(f32[16,2,8,512]{3,2,1,0:T(8,128)} %recorded_ref.3) | copy-start | bytes 1572868
  14.5 31.2 %copy-start.7 = (f32[16]{0:T(128)S(1)}, f32[16]{0:T(128)}, u32[]{:S(2)}) copy-start(f32[16]{0:T(128)} %steps_ref.3) | copy-start | bytes 196
  55.3 19.0 %copy-start.3 = (bf16[256,256]{1,0:T(8,128)(2,1)S(1)}, bf16[256,256]{1,0:T(8,128)(2,1)}, u32[]{:S(2)}) copy-start(bf16[256,256]{1,0:T(8,128)(2,1)} %constant.24.clone.refs_1_) | copy-start | bytes 393220
  55.3 19.0 %copy-start.4 = (bf16[256,256]{1,0:T(8,128)(2,1)S(1)}, bf16[256,256]{1,0:T(8,128)(2,1)}, u32[]{:S(2)}) copy-start(bf16[256,256]{1,0:T(8,128)(2,1)} %constant.25.clone.refs_2_) | copy-start | bytes 393220
  55.3 19.0 %copy-start.5 = (bf16[256,256]{1,0:T(8,128)(2,1)S(1)}, bf16[256,256]{1,0:T(8,128)(2,1)}, u32[]{:S(2)}) copy-start(bf16[256,256]{1,0:T(8,128)(2,1)} %constant.26.clone.refs_3_) | copy-start | bytes 393220
  55.3 19.0 %copy-start.6 = (bf16[256,256]{1,0:T(8,128)(2,1)S(1)}, bf16[256,256]{1,0:T(8,128)(2,1)}, u32[]{:S(2)}) copy-start(bf16[256,256]{1,0:T(8,128)(2,1)} %constant.27.clone.refs_4_) | copy-start | bytes 393220
  55.3 19.0 %copy-start.8 = (f32[8]{0:T(128)S(1)}, f32[8]{0:T(128)}, u32[]{:S(2)}) copy-start(f32[8]{0:T(128)} %refs_0_.3) | copy-start | bytes 100
  78.7 1.3 copy-start.1
  80.0 18.9 %all-to-all-start.2 = ((bf16[8,16,16,256]{3,2,1,0:T(8,128)(2,1)}), bf16[8,16,16,256]{3,2,1,0:T(8,128)(2,1)S(1)}, u32[]{:S(2)}, u32[]{:S(2)}) async-start(bf16[8,16,16,256]{3,2,1,0:T(8,128)(2,1)} %get-tuple-element.7), calls=%async_computation.2 | async-start | bytes 2097152 | tf_op jit(solution)/shard_map/all_to_all | solution.py:400
  163.3 20.9 %copy-start.2 = (f32[8,256,256]{2,1,0:T(8,128)S(1)}, f32[8,256,256]{2,1,0:T(8,128)}, u32[]{:S(2)}) copy-start(f32[8,256,256]{2,1,0:T(8,128)} %copy-done.1) | copy-start | bytes 6291460

commit v2 on v1

--- a/solution.py
+++ b/solution.py
@@ -224,7 +224,7 @@
         store_duals(out_ref, at, duals, peers)
 
 
-def spread_kernel(steps_ref, right_ref, duals_ref, out_ref):
+def spread_kernel(base, steps_ref, right_ref, duals_ref, out_ref):
     freqs, rows, cols, _, rank, width = right_ref.shape
     peers, _, both, share = duals_ref.shape
     rows_each = rows // peers
@@ -246,7 +246,7 @@
         total = 0.0
         for row in range(rows):
             total += nn_dot(wide[row], right_ref[at, row].reshape(cols * group, width))
-        step = steps_ref[pl.program_id(0) * freqs + at]
+        step = steps_ref[base + at]
         out_ref[:, at] = (total * step).astype(jnp.bfloat16).reshape(cols, 2 * virtual, width)
 
 
@@ -284,25 +284,18 @@
     return high, (values - high.astype(jnp.float32)).astype(jnp.bfloat16)
 
 
-def shrink_kernel(second, *refs):
-    if second:
-        (levels_ref, to_high, to_low, back_high, back_low, field_ref, kept_ref, out_ref,
-         wide, packed) = refs
-    else:
-        (levels_ref, to_high, to_low, back_high, back_low, field_ref, out_ref, kept_ref,
-         wide, packed) = refs
+def shrink_kernel(second, levels_ref, tables, field_ref, kept_ref, out_ref, wide, packed):
+    to_high, to_low, back_high, back_low = tables
     virtual = levels_ref.shape[0]
-    peers, freqs, rows, width = field_ref.shape
-    times = to_high.shape[0]
-    lines = peers * freqs * 2
+    width = field_ref.shape[-1]
+    times, lines = to_high.shape
     halves = [slice(at, at + 128) for at in range(0, width, 128)]
     for half, lanes in enumerate(halves):
         wide[half] = (
-            field_ref[:, :, :, lanes].astype(jnp.float32).reshape(lines * virtual, 128)
-        )
-    if not second:
-        odd = lax.broadcasted_iota(jnp.int32, (times, width), 0) % 2
-        turn = jnp.where(odd == 0, 1.0, -1.0)
+            field_ref[:, :, :, :, lanes].astype(jnp.float32).reshape(lines * virtual, 128)
+        )
+    odd = lax.broadcasted_iota(jnp.int32, (times, width), 0) % 2
+    turn = jnp.where(odd == 0, 1.0, -1.0)
     for source in range(virtual):
         own = pl.ds(source, lines, stride=virtual)
         spectrum = jnp.concatenate(
@@ -312,7 +305,7 @@
         if second:
             signal += kept_ref[source]
         level = levels_ref[source]
-        shrunk = signal - jnp.clip(signal, -level, level)
+        shrunk = signal - jnp.minimum(jnp.maximum(signal, -level), level)
         if not second:
             mean = jnp.sum(shrunk * turn, 0, keepdims=True) * (1.0 / times)
             kept_ref[source] = shrunk - turn * mean
@@ -323,9 +316,174 @@
         for half, lanes in enumerate(halves):
             packed[half, own, :] = freq[:, lanes]
     for half, lanes in enumerate(halves):
-        out_ref[:, :, :, lanes] = (
-            packed[half].astype(jnp.bfloat16).reshape(peers, freqs, rows, 128)
-        )
+        out_ref[:, :, :, :, lanes] = (
+            packed[half].astype(jnp.bfloat16).reshape(out_ref.shape[:-1] + (128,))
+        )
+
+
+class Exchange:
+    def __init__(self, axis, send, recv, send_sem, recv_sem):
+        self.axis, self.send, self.recv = axis, send, recv
+        self.send_sem, self.recv_sem = send_sem, recv_sem
+        self.size = send.shape[0]
+        self.me = lax.axis_index(axis)
+
+    def peers(self):
+        return [lax.rem(self.me + step, self.size) for step in range(1, self.size)]
+
+    def copy(self, block, peer, source):
+        return pltpu.make_async_remote_copy(
+            src_ref=self.send.at[peer, block],
+            dst_ref=self.recv.at[source, block],
+            send_sem=self.send_sem.at[block, peer],
+            recv_sem=self.recv_sem.at[block, source],
+            device_id={self.axis: peer},
+            device_id_type=pl.DeviceIdType.MESH,
+        )
+
+    def start(self, block):
+        for peer in self.peers():
+            self.copy(block, peer, self.me).start()
+        self.recv[self.me, block] = self.send[self.me, block]
+
+    def start_all(self):
+        @pl.loop(0, self.send.shape[1])
+        def _(block):
+            self.start(block)
+
+    def wait(self, block):
+        for peer in self.peers():
+            self.copy(block, peer, peer).wait_recv()
+
+    def wait_all(self):
+        @pl.loop(0, self.send.shape[1])
+        def _(block):
+            self.wait(block)
+
+    def finish(self):
+        @pl.loop(0, self.send.shape[1])
+        def _(block):
+            for peer in self.peers():
+                self.copy(block, peer, self.me).wait_send()
+
+
+def stages(blocks):
+    lag = LAG
+    first_shrink = blocks + lag
+    second_shrink = first_shrink + blocks + 2 * lag
+    return lag, first_shrink, second_shrink, second_shrink + blocks
+
+
+def whole_kernel(
+    levels_ref, steps_ref, to_high, to_low, back_high, back_low,
+    left_ref, recorded_ref, weight_left_ref, right_a_ref, weight_right_ref, right_b_ref,
+    out_ref,
+    tile_send, tile_recv, freq_send, freq_recv, tile_ssem, tile_rsem, freq_ssem, freq_rsem,
+    kept, wide, packed,
+):
+    step = pl.program_id(0)
+    block = left_ref.shape[0]
+    blocks = tile_send.shape[2]
+    lag, first_shrink, second_shrink, last = stages(blocks)
+    tables = (to_high, to_low, back_high, back_low)
+    over_tile = [
+        Exchange("tile", tile_send.at[n], tile_recv.at[n], tile_ssem.at[n], tile_rsem.at[n])
+        for n in range(tile_send.shape[0])
+    ]
+    over_freq = [
+        Exchange("freq", freq_send.at[n], freq_recv.at[n], freq_ssem.at[n], freq_rsem.at[n])
+        for n in range(freq_send.shape[0])
+    ]
+
+    def span(start):
+        return (step >= start) & (step < start + blocks)
+
+    @pl.when(step == 0)
+    def _():
+        barrier = pltpu.get_barrier_semaphore()
+        count = 0
+        for exchange in (over_tile[0], over_freq[0]):
+            for peer in exchange.peers():
+                pl.semaphore_signal(
+                    barrier, inc=1, device_id={exchange.axis: peer},
+                    device_id_type=pl.DeviceIdType.MESH,
+                )
+                count += 1
+        pl.semaphore_wait(barrier, count)
+
+    @pl.when(span(0))
+    def _():
+        dual_kernel(left_ref, recorded_ref, weight_left_ref, over_tile[0].send.at[:, step])
+        over_tile[0].start(step)
+
+    def spread(start, tiles, freqs):
+        @pl.when(span(start))
+        def _():
+            b = step - start
+            tiles.wait(b)
+            spread_kernel(
+                b * block, steps_ref, right_b_ref, tiles.recv.at[:, b], freqs.send.at[:, b]
+            )
+            freqs.start(b)
+
+    spread(lag, over_tile[0], over_freq[0])
+
+    @pl.when(step == first_shrink)
+    def _():
+        over_freq[0].wait_all()
+        shrink_kernel(
+            False, levels_ref, tables, over_freq[0].recv, kept, over_freq[1].send, wide, packed
+        )
+        over_freq[1].start_all()
+
+    @pl.when(span(first_shrink))
+    def _():
+        b = step - first_shrink
+        over_freq[1].wait(b)
+        project_kernel(
+            right_a_ref, over_freq[1].recv.at[:, b], weight_right_ref,
+            over_tile[1].send.at[:, b],
+        )
+        over_tile[1].start(b)
+
+    @pl.when(span(first_shrink + lag))
+    def _():
+        b = step - first_shrink - lag
+        over_tile[1].wait(b)
+        image_kernel(
+            left_ref, over_tile[1].recv.at[:, b], recorded_ref, weight_left_ref,
+            over_tile[2].send.at[:, b],
+        )
+        over_tile[2].start(b)
+
+    spread(first_shrink + 2 * lag, over_tile[2], over_freq[2])
+
+    @pl.when(step == second_shrink)
+    def _():
+        over_freq[2].wait_all()
+        shrink_kernel(
+            True, levels_ref, tables, over_freq[2].recv, kept, over_freq[3].send, wide, packed
+        )
+        over_freq[3].start_all()
+
+    @pl.when(span(second_shrink))
+    def _():
+        b = step - second_shrink
+        over_freq[3].wait(b)
+        peers, _, at_once, rows, width = over_freq[3].recv.shape
+        for at in range(at_once):
+            for peer in range(peers):
+                out_ref[at, :, peer * width : (peer + 1) * width] = over_freq[3].recv[
+                    peer, b, at
+                ].astype(jnp.float32)
+
+    @pl.when(step == last - 1)
+    def _():
+        for exchange in over_tile + over_freq:
+            exchange.finish()
+
+
+LAG = 2
 
 
 def table_parts():
@@ -346,9 +504,6 @@
 
 def smem():
     return pl.BlockSpec(memory_space=pltpu.SMEM)
-
-
-PARAMS = pltpu.CompilerParams(vmem_limit_bytes=48 << 20, dimension_semantics=("arbitrary",))
 
 
 def per_device(
@@ -362,97 +517,89 @@
     lines = rows_here * virtual
     tile_pos = lax.axis_index("tile")
     block = 2 if freqs % 2 == 0 else 1
-    grid = (freqs // block,)
-
-    weights = slot_weights(tile_ranks, tile_scales, rank)
-    weights = jnp.broadcast_to(
-        weights[:, :, :, None, :], (freqs, row_tiles, col_tiles, 2, rank)
-    ).reshape(freqs, row_tiles, col_tiles * 2 * rank)
-    weights_left = lax.dynamic_slice_in_dim(weights, tile_pos * rows_here, rows_here, 1)
-    weights_right = lax.dynamic_slice_in_dim(weights, tile_pos * share, share, 2)
-
-    def by_freq(array):
+    blocks = freqs // block
+    lag, first_shrink, second_shrink, steps = stages(blocks)
+
+    def slot_lanes(row_at, rows, col_at, cols):
+        ranks = tile_ranks.astype(jnp.float32)
+        scales = tile_scales[:, 0] * tile_scales[:, 1]
+        cut = lambda array: lax.dynamic_slice(array, (0, row_at, col_at), (freqs, rows, cols))
+        lanes = np.arange(cols * 2 * rank)
+        spread_out = jnp.asarray(
+            (lanes[None, :] // (2 * rank) == np.arange(cols)[:, None]).astype(np.float32)
+        )
+        widen = lambda array: jnp.einsum(
+            "fij,jl->fil", cut(array), spread_out, precision=lax.Precision.HIGHEST
+        )
+        slot = (jnp.arange(cols * 2 * rank) % rank).astype(jnp.float32)
+        return jnp.where(slot < widen(ranks) - 0.5, widen(scales), 0.0)
+
+    weights_left = slot_lanes(tile_pos * rows_here, rows_here, 0, col_tiles)
+    weights_right = slot_lanes(0, row_tiles, tile_pos * cols_here, cols_here)
+
+    def spec(array, index):
         rest = array.shape[1:]
-        return pl.BlockSpec((block,) + rest, lambda f: (f,) + (0,) * len(rest))
-
-    def by_second(shape):
-        return pl.BlockSpec((shape[0], block) + shape[2:], lambda f: (0, f, 0, 0))
-
-    coef_shape = (tile_size, freqs, lines, share)
-    field_shape = (cols_here, freqs, 2 * virtual, width)
-    coef_type = jax.ShapeDtypeStruct(coef_shape, jnp.bfloat16)
-    field_type = jax.ShapeDtypeStruct(field_shape, jnp.bfloat16)
-
-    def spread(duals):
-        return pl.pallas_call(
-            spread_kernel,
-            out_shape=field_type,
-            grid=grid,
-            in_specs=[smem(), by_freq(right_factor), by_second(coef_shape)],
-            out_specs=by_second(field_shape),
-            compiler_params=PARAMS,
-        )(step_sizes, right_factor, duals)
-
-    def over_tile(array):
-        return lax.all_to_all(array, "tile", split_axis=0, concat_axis=0, tiled=True)
-
-    def over_freq(array):
-        return lax.all_to_all(array, "freq", split_axis=0, concat_axis=0, tiled=True)
-
-    times = 2 * F
-    kept_type = jax.ShapeDtypeStruct((virtual, times, width), jnp.float32)
-    tables = table_parts()
-    scratch = [pltpu.VMEM((width // 128, times * virtual, 128), jnp.float32)] * 2
-
-    duals = pl.pallas_call(
-        dual_kernel,
-        out_shape=coef_type,
-        grid=grid,
-        in_specs=[by_freq(left_factor), by_freq(recorded), by_freq(weights_left)],
-        out_specs=by_second(coef_shape),
-        compiler_params=PARAMS,
-    )(left_factor, recorded, weights_left)
-    gradient = over_freq(spread(over_tile(duals)))
-    first, kept = pl.pallas_call(
-        functools.partial(shrink_kernel, False),
-        out_shape=[field_type, kept_type],
-        in_specs=[smem()] + [vmem()] * 5,
-        out_specs=[vmem(), vmem()],
-        scratch_shapes=scratch,
-        compiler_params=pltpu.CompilerParams(vmem_limit_bytes=48 << 20),
-    )(thresholds, *tables, gradient)
-    coefs = pl.pallas_call(
-        project_kernel,
-        out_shape=coef_type,
-        grid=grid,
-        in_specs=[by_freq(right_factor), by_second(field_shape), by_freq(weights_right)],
-        out_specs=by_second(coef_shape),
-        compiler_params=PARAMS,
-    )(right_factor, over_freq(first), weights_right)
-    duals = pl.pallas_call(
-        image_kernel,
-        out_shape=coef_type,
-        grid=grid,
-        in_specs=[
-            by_freq(left_factor),
-            by_second(coef_shape),
-            by_freq(recorded),
-            by_freq(weights_left),
+        return pl.BlockSpec((block,) + rest, lambda s: (index(s),) + (0,) * len(rest))
+
+    def within(at):
+        return jnp.minimum(jnp.maximum(at, 0), blocks - 1)
+
+    def left_index(s):
+        return jnp.where(s < blocks, s, within(s - first_shrink - lag))
+
+    def project_index(s):
+        return within(s - first_shrink)
+
+    def spread_index(s):
+        return jnp.where(s < first_shrink, within(s - lag), within(s - first_shrink - 2 * lag))
+
+    def out_index(s):
+        return within(s - second_shrink)
+
+    out_shape = (freqs, 2 * virtual, cols_here * width)
+    dma = pltpu.SemaphoreType.DMA
+    tile_buffer = pltpu.VMEM((3, tile_size, blocks, block, lines, share), jnp.bfloat16)
+    freq_buffer = pltpu.VMEM((4, cols_here, blocks, block, 2 * virtual, width), jnp.bfloat16)
+    wide = pltpu.VMEM((width // 128, 2 * F * virtual, 128), jnp.float32)
+    estimate = pl.pallas_call(
+        whole_kernel,
+        out_shape=jax.ShapeDtypeStruct(out_shape, jnp.float32),
+        grid=(steps,),
+        in_specs=[smem(), smem()]
+        + [vmem()] * 4
+        + [
+            spec(left_factor, left_index),
+            spec(recorded, left_index),
+            spec(weights_left, left_index),
+            spec(right_factor, project_index),
+            spec(weights_right, project_index),
+            spec(right_factor, spread_index),
         ],
-        out_specs=by_second(coef_shape),
-        compiler_params=PARAMS,
-    )(left_factor, over_tile(coefs), recorded, weights_left)
-    gradient = over_freq(spread(over_tile(duals)))
-    estimate = pl.pallas_call(
-        functools.partial(shrink_kernel, True),
-        out_shape=field_type,
-        in_specs=[smem()] + [vmem()] * 6,
-        out_specs=vmem(),
-        scratch_shapes=scratch,
-        compiler_params=pltpu.CompilerParams(vmem_limit_bytes=48 << 20),
-    )(thresholds, *tables, gradient, kept)
-    arrived = over_freq(estimate).astype(jnp.float32)
-    return arrived.transpose(1, 2, 0, 3).reshape(freqs, 2, virtual, cols_here * width)
+        out_specs=pl.BlockSpec((block,) + out_shape[1:], lambda s: (out_index(s), 0, 0)),
+        scratch_shapes=[
+            tile_buffer,
+            tile_buffer,
+            freq_buffer,
+            freq_buffer,
+            dma((3, blocks, tile_size)),
+            dma((3, blocks, tile_size)),
+            dma((4, blocks, cols_here)),
+            dma((4, blocks, cols_here)),
+            pltpu.VMEM((virtual, 2 * F, width), jnp.float32),
+            wide,
+            wide,
+        ],
+        compiler_params=pltpu.CompilerParams(
+            vmem_limit_bytes=56 << 20,
+            dimension_semantics=("arbitrary",),
+            collective_id=0,
+            has_side_effects=True,
+        ),
+    )(
+        thresholds, step_sizes, *table_parts(), left_factor, recorded, weights_left,
+        right_factor, weights_right, right_factor,
+    )
+    return estimate.reshape(freqs, 2, virtual, cols_here * width)
 
 
 def either(*arrays):

time: 210 us -> 105 us (0.50)
  blocking collectives: 108 us -> 0 us
  Pallas kernels: 61.9 us -> 94.1 us
  waiting for transfers between devices: 15.3 us -> 0 us
  local copies, waits for them, and re-layouts: 16.2 us -> 3.23 us
  matrix products: 0 us -> 4.95 us
  starting transfers between devices: 3.56 us -> 0 us
    all_to_all x6 -> x0, blocking collectives: 108 us -> none  [the longest x3 57.6 us: over_freq(): lax.all_to_all(array, 'freq', split_axis=0, concat_axis=0, tiled=True)]
    pallas_call x7 -> x1, Pallas kernels: 61.9 us -> 94.1 us  [per_device(): pl.pallas_call(whole_kernel, out_shape=jax.ShapeDtypeStruct(out_shape, jn...]
    all_to_all x1 -> x0, waiting for transfers between devices: 15.3 us -> none  [over_freq(): lax.all_to_all(array, 'freq', split_axis=0, concat_axis=0, tiled=True)]
    reshape x3 -> x0, local copies, waits for them, and re-layouts: 11.1 us -> none  [the longest x1 7.95 us: per_device(): weights = jnp.broadcast_to(weights[:, :, :, None, :], (freqs, row_tiles,...]
    dot_general x0 -> x4, matrix products: none -> 4.95 us  [slot_lanes(): jnp.einsum('fij,jl->fil', cut(array), spread_out, precision=lax.Precision...]
    broadcast_in_dim x1 -> x0, local copies, waits for them, and re-layouts: 3.64 us -> none  [per_device(): jnp.broadcast_to(weights[:, :, :, None, :], (freqs, row_tiles, col_tiles,...]
    all_to_all x1 -> x0, starting transfers between devices: 3.56 us -> none  [over_freq(): lax.all_to_all(array, 'freq', split_axis=0, concat_axis=0, tiled=True)]
  transfers between devices with their start and end apart: 1 -> 0, of which waited for: 1 -> 0; matrix products, arithmetic and copies ran while one was open for 0% -> 0% of each run, Pallas kernels for 0% -> 0%
where the time goes in v2:
time: 105 us
  Pallas kernels  94.1 us (90%)
  matrix products  4.95 us (5%)
  local copies, waits for them, and re-layouts  3.23 us (3%)
  other arithmetic  2.61 us (2%)
    pallas_call x1, Pallas kernels, per_device(): pl.pallas_call(whole_kernel, out_shape=jax.ShapeDtypeStruct(out_shape, jn...  94.1 us
    dot_general x4, matrix products, slot_lanes(): jnp.einsum('fij,jl->fil', cut(array), spread_out, precision=lax.Precision...  4.95 us
    unnamed x1, local copies, waits for them, and re-layouts  3.14 us

profile of v2, /device:TPU:0, one launch (start us, length us, event | category | flops | bytes accessed | tf_op | source)
XLA Modules:
  0.0 104.9 jit_solution(9290584011123400611)
XLA Ops:
  0.0 0.9 copy_convert_fusion
  0.9 0.9 slice_multiply_fusion
  1.8 0.1 constant_dynamic-slice_fusion
  1.9 1.0 fusion
  2.8 1.7 %convolution_select_fusion.weight_right_ref = f32[16,8,256]{2,1,0:T(8,128)} fusion(pred[16,8,256]{2,1,0:T(8,128)(4,1)S(1)} %fusion, f32[8,256,1]{1,0,2:T(8,128)} %constant.65, f32[16,1,8,32]{3,2,1,0:T(8,128)S(1)} %slice_multiply_fusion, s32[]{:T(128)S(6)} %select_n.41), kind=kOutput, calls=%fused_computation | convolution fusion | flops 3178496 | bytes 188420 | tf_op jit(solution)/shard_map/fij,jl->fil/dot_general | solution.py:531
  4.5 1.2 %fusion.7 = f32[16,2,1024]{2,0,1:T(8,128)S(1)} fusion(f32[32,1024,1]{1,0,2:T(8,128)} %constant.64, f32[16,8,32]{2,0,1:T(8,128)S(1)} %copy_convert_fusion, s32[]{:T(128)S(6)} %select_n.38), kind=kOutput, calls=%fused_computation.13 | convolution fusion | flops 12582912 | bytes 278532 | tf_op jit(solution)/shard_map/fij,jl->fil/dot_general | solution.py:531
  5.7 1.2 %fusion.4 = f32[16,2,1024]{2,0,1:T(8,128)S(1)} fusion(f32[32,1024,1]{1,0,2:T(8,128)} %constant.64, f32[16,1,2,32]{3,2,1,0:T(2,128)S(1)} %constant_dynamic-slice_fusion.1), kind=kOutput, calls=%fused_computation.10 | convolution fusion | flops 12582912 | bytes 266240 | tf_op jit(solution)/shard_map/fij,jl->fil/dot_general | solution.py:531
  6.8 0.9 compare_select_fusion.weight_left_ref
  7.7 94.1 %shard_map.127 = f32[16,16,2048]{2,1,0:T(8,128)} custom-call(f32[8]{0:T(128)} %levels_ref.1, f32[16]{0:T(128)} %steps_ref.1, bf16[256,256]{1,0:T(8,128)(2,1)} %constant.59.clone.to_high, bf16[256,256]{1,0:T(8,128)(2,1)} %constant.60.clone.to_low, bf16[256,256]{1,0:T(8,128)(2,1)} %constant.61.clone.back_high, bf16[256,256]{1,0:T(8,128)(2,1)} %constant.62.clone.back_low, ...), custom_call_target="tpu_custom_call" | custom-call | tf_op jit(solution)/shard_map/pallas_call | solution.py:564
  101.8 3.1 %copy.31 = f32[16,2,8,2048]{3,2,1,0:T(8,128)} copy(f32[16,2,8,2048]{3,2,1,0:T(8,128)} %bitcast.13) | data formatting | bytes 4194304
  (3 shorter events, 0.0 us)

commit v3 on v2

--- a/solution.py
+++ b/solution.py
@@ -188,7 +188,7 @@
         out_ref[peer, at] = together[:, peer * width : (peer + 1) * width].astype(jnp.bfloat16)
 
 
-def dual_kernel(left_ref, recorded_ref, weight_ref, out_ref):
+def dual_kernel(base, left_ref, recorded_ref, weight_ref, out_ref):
     freqs, rows, cols, _, rank, width = left_ref.shape
     peers = out_ref.shape[0]
     for at in range(freqs):
@@ -197,11 +197,11 @@
             left_rows = left_ref[at, row].reshape(cols * 2 * rank, width)
             part = recorded_ref[at, :, :, row * width : (row + 1) * width]
             field = part.reshape(-1, width)
-            duals.append(dual_of(left_rows, field, weight_ref[at, row : row + 1], rank))
+            duals.append(dual_of(left_rows, field, weight_ref[pl.ds((base + at) * rows + row, 1), :], rank))
         store_duals(out_ref, at, duals, peers)
 
 
-def image_kernel(left_ref, coefs_ref, recorded_ref, weight_ref, out_ref):
+def image_kernel(base, left_ref, coefs_ref, recorded_ref, weight_ref, out_ref):
     freqs, rows, cols, _, rank, width = left_ref.shape
     peers = coefs_ref.shape[0]
     share = cols // peers * 2 * rank
@@ -220,7 +220,7 @@
                 image += nn_dot(both, left_rows[peer * share : (peer + 1) * share])
             part = recorded_ref[at, :, :, row * width : (row + 1) * width]
             field = part.reshape(-1, width) - image
-            duals.append(dual_of(left_rows, field, weight_ref[at, row : row + 1], rank))
+            duals.append(dual_of(left_rows, field, weight_ref[pl.ds((base + at) * rows + row, 1), :], rank))
         store_duals(out_ref, at, duals, peers)
 
 
@@ -250,7 +250,7 @@
         out_ref[:, at] = (total * step).astype(jnp.bfloat16).reshape(cols, 2 * virtual, width)
 
 
-def project_kernel(right_ref, field_ref, weight_ref, out_ref):
+def project_kernel(base, right_ref, field_ref, weight_ref, out_ref):
     freqs, rows, cols, _, rank, width = right_ref.shape
     peers, _, both, share = out_ref.shape
     rows_each = rows // peers
@@ -275,7 +275,8 @@
                         piece = rows_of if step == 0 else jnp.where(owner == step, rows_of, piece)
                     pieces.append(piece)
                 picked = jnp.concatenate(pieces, 1)
-                coefs.append(adjoint_rows(picked, rank) * weight_ref[at, row : row + 1])
+                weight = weight_ref[pl.ds((base + at) * rows + row, 1), :]
+                coefs.append(adjoint_rows(picked, rank) * weight)
             out_ref[peer, at] = jnp.concatenate(coefs, 0).astype(jnp.bfloat16)
 
 
@@ -376,13 +377,15 @@
 
 def whole_kernel(
     levels_ref, steps_ref, to_high, to_low, back_high, back_low,
-    left_ref, recorded_ref, weight_left_ref, right_a_ref, weight_right_ref, right_b_ref,
+    left_hbm, right_hbm, recorded_ref, cells_left_ref, cells_right_ref,
     out_ref,
+    left, right, left_sem, right_sem, weight_left_ref, weight_right_ref,
     tile_send, tile_recv, freq_send, freq_recv, tile_ssem, tile_rsem, freq_ssem, freq_rsem,
     kept, wide, packed,
 ):
     step = pl.program_id(0)
-    block = left_ref.shape[0]
+    block = left.shape[1]
+    rank = left.shape[5]
     blocks = tile_send.shape[2]
     lag, first_shrink, second_shrink, last = stages(blocks)
     tables = (to_high, to_low, back_high, back_low)
@@ -398,6 +401,24 @@
     def span(start):
         return (step >= start) & (step < start + blocks)
 
+    def fetch(source, target, sem, at):
+        return pltpu.make_async_copy(
+            source.at[pl.ds(at * block, block)], target.at[at], sem.at[at]
+        )
+
+    def fetch_both(at):
+        fetch(left_hbm, left, left_sem, at).start()
+        fetch(right_hbm, right, right_sem, at).start()
+
+    @pl.when(step == 0)
+    def _():
+        for at in range(min(AHEAD, blocks)):
+            fetch_both(at)
+
+    @pl.when(step + AHEAD < blocks)
+    def _():
+        fetch_both(step + AHEAD)
+
     @pl.when(step == 0)
     def _():
         barrier = pltpu.get_barrier_semaphore()
@@ -409,20 +430,28 @@
                     device_id_type=pl.DeviceIdType.MESH,
                 )
                 count += 1
+        lane_weights(cells_left_ref, weight_left_ref, rank)
+        lane_weights(cells_right_ref, weight_right_ref, rank)
         pl.semaphore_wait(barrier, count)
 
     @pl.when(span(0))
     def _():
-        dual_kernel(left_ref, recorded_ref, weight_left_ref, over_tile[0].send.at[:, step])
+        fetch(left_hbm, left, left_sem, step).wait()
+        dual_kernel(
+            step * block, left.at[step], recorded_ref, weight_left_ref,
+            over_tile[0].send.at[:, step],
+        )
         over_tile[0].start(step)
 
     def spread(start, tiles, freqs):
         @pl.when(span(start))
         def _():
             b = step - start
+            if start == lag:
+                fetch(right_hbm, right, right_sem, b).wait()
             tiles.wait(b)
             spread_kernel(
-                b * block, steps_ref, right_b_ref, tiles.recv.at[:, b], freqs.send.at[:, b]
+                b * block, steps_ref, right.at[b], tiles.recv.at[:, b], freqs.send.at[:, b]
             )
             freqs.start(b)
 
@@ -441,7 +470,7 @@
         b = step - first_shrink
         over_freq[1].wait(b)
         project_kernel(
-            right_a_ref, over_freq[1].recv.at[:, b], weight_right_ref,
+            b * block, right.at[b], over_freq[1].recv.at[:, b], weight_right_ref,
             over_tile[1].send.at[:, b],
         )
         over_tile[1].start(b)
@@ -451,7 +480,7 @@
         b = step - first_shrink - lag
         over_tile[1].wait(b)
         image_kernel(
-            left_ref, over_tile[1].recv.at[:, b], recorded_ref, weight_left_ref,
+            b * block, left.at[b], over_tile[1].recv.at[:, b], recorded_ref, weight_left_ref,
             over_tile[2].send.at[:, b],
         )
         over_tile[2].start(b)
@@ -475,7 +504,7 @@
             for peer in range(peers):
                 out_ref[at, :, peer * width : (peer + 1) * width] = over_freq[3].recv[
                     peer, b, at
-                ].astype(jnp.float32)
+                ]
 
     @pl.when(step == last - 1)
     def _():
@@ -484,6 +513,19 @@
 
 
 LAG = 2
+AHEAD = 3
+
+
+def lane_weights(cells_ref, out_ref, rank):
+    _, rows, tiles = cells_ref.shape
+    lanes = out_ref.shape[1]
+    owner = lax.broadcasted_iota(jnp.int32, (tiles, lanes), 1) // (2 * rank)
+    pick = (owner == lax.broadcasted_iota(jnp.int32, (tiles, lanes), 0)).astype(jnp.float32)
+    widen = lambda values: jnp.dot(
+        values, pick, precision=lax.Precision.HIGHEST, preferred_element_type=jnp.float32
+    )
+    slot = (lane_ids(rows, lanes) % rank).astype(jnp.float32)
+    out_ref[...] = jnp.where(slot < widen(cells_ref[0]) - 0.5, widen(cells_ref[1]), 0.0)
 
 
 def table_parts():
@@ -520,22 +562,13 @@
     blocks = freqs // block
     lag, first_shrink, second_shrink, steps = stages(blocks)
 
-    def slot_lanes(row_at, rows, col_at, cols):
-        ranks = tile_ranks.astype(jnp.float32)
-        scales = tile_scales[:, 0] * tile_scales[:, 1]
-        cut = lambda array: lax.dynamic_slice(array, (0, row_at, col_at), (freqs, rows, cols))
-        lanes = np.arange(cols * 2 * rank)
-        spread_out = jnp.asarray(
-            (lanes[None, :] // (2 * rank) == np.arange(cols)[:, None]).astype(np.float32)
-        )
-        widen = lambda array: jnp.einsum(
-            "fij,jl->fil", cut(array), spread_out, precision=lax.Precision.HIGHEST
-        )
-        slot = (jnp.arange(cols * 2 * rank) % rank).astype(jnp.float32)
-        return jnp.where(slot < widen(ranks) - 0.5, widen(scales), 0.0)
-
-    weights_left = slot_lanes(tile_pos * rows_here, rows_here, 0, col_tiles)
-    weights_right = slot_lanes(0, row_tiles, tile_pos * cols_here, cols_here)
+    cells = jnp.stack(
+        [tile_ranks.astype(jnp.float32), tile_scales[:, 0] * tile_scales[:, 1]]
+    )
+    cells_left = lax.dynamic_slice_in_dim(cells, tile_pos * rows_here, rows_here, 2)
+    cells_left = cells_left.reshape(2, freqs * rows_here, col_tiles)
+    cells_right = lax.dynamic_slice_in_dim(cells, tile_pos * cols_here, cols_here, 3)
+    cells_right = cells_right.reshape(2, freqs * row_tiles, cols_here)
 
     def spec(array, index):
         rest = array.shape[1:]
@@ -546,12 +579,6 @@
 
     def left_index(s):
         return jnp.where(s < blocks, s, within(s - first_shrink - lag))
-
-    def project_index(s):
-        return within(s - first_shrink)
-
-    def spread_index(s):
-        return jnp.where(s < first_shrink, within(s - lag), within(s - first_shrink - 2 * lag))
 
     def out_index(s):
         return within(s - second_shrink)
@@ -563,20 +590,20 @@
     wide = pltpu.VMEM((width // 128, 2 * F * virtual, 128), jnp.float32)
     estimate = pl.pallas_call(
         whole_kernel,
-        out_shape=jax.ShapeDtypeStruct(out_shape, jnp.float32),
+        out_shape=jax.ShapeDtypeStruct(out_shape, jnp.bfloat16),
         grid=(steps,),
         in_specs=[smem(), smem()]
         + [vmem()] * 4
-        + [
-            spec(left_factor, left_index),
-            spec(recorded, left_index),
-            spec(weights_left, left_index),
-            spec(right_factor, project_index),
-            spec(weights_right, project_index),
-            spec(right_factor, spread_index),
-        ],
+        + [pl.BlockSpec(memory_space=pl.ANY)] * 2
+        + [spec(recorded, left_index), vmem(), vmem()],
         out_specs=pl.BlockSpec((block,) + out_shape[1:], lambda s: (out_index(s), 0, 0)),
         scratch_shapes=[
+            pltpu.VMEM((blocks, block) + left_factor.shape[1:], jnp.bfloat16),
+            pltpu.VMEM((blocks, block) + right_factor.shape[1:], jnp.bfloat16),
+            dma((blocks,)),
+            dma((blocks,)),
+            pltpu.VMEM((freqs * rows_here, col_tiles * 2 * rank), jnp.float32),
+            pltpu.VMEM((freqs * row_tiles, share), jnp.float32),
             tile_buffer,
             tile_buffer,
             freq_buffer,
@@ -590,16 +617,16 @@
             wide,
         ],
         compiler_params=pltpu.CompilerParams(
-            vmem_limit_bytes=56 << 20,
+            vmem_limit_bytes=58 << 20,
             dimension_semantics=("arbitrary",),
             collective_id=0,
             has_side_effects=True,
         ),
     )(
-        thresholds, step_sizes, *table_parts(), left_factor, recorded, weights_left,
-        right_factor, weights_right, right_factor,
+        thresholds, step_sizes, *table_parts(), left_factor, right_factor, recorded,
+        cells_left, cells_right,
     )
-    return estimate.reshape(freqs, 2, virtual, cols_here * width)
+    return estimate.astype(jnp.float32).reshape(freqs, 2, virtual, cols_here * width)
 
 
 def either(*arrays):

time: 105 us -> 96.5 us (0.919)
  matrix products: 4.95 us -> 0 us
  Pallas kernels: 94.1 us -> 90.3 us
  other arithmetic: 2.61 us -> 5.9 us
  local copies, waits for them, and re-layouts: 3.23 us -> 0 us
    dot_general x4 -> x0, matrix products: 4.95 us -> none  [slot_lanes(): jnp.einsum('fij,jl->fil', cut(array), spread_out, precision=lax.Precision...]
    pallas_call x1, Pallas kernels: 94.1 us -> 90.3 us  [per_device(): pl.pallas_call(whole_kernel, out_shape=jax.ShapeDtypeStruct(out_shape, jn...]
    reshape x0 -> x2, other arithmetic: none -> 3.55 us  [the longest x1 2.79 us: per_device(): estimate.astype(jnp.float32).reshape(freqs, 2, virtual, cols_here * width)]
    unnamed x1 -> x0, local copies, waits for them, and re-layouts: 3.14 us -> none
    another operation x0 -> x2, other arithmetic: none -> 1.47 us  [per_device(): jnp.stack([tile_ranks.astype(jnp.float32), tile_scales[:, 0] * tile_scale...]
where the time goes in v3:
time: 96.5 us; the launch traced here: 96.3 us
  Pallas kernels  90.3 us (94%)
  other arithmetic  5.9 us (6%)
    pallas_call x1, Pallas kernels, per_device(): pl.pallas_call(whole_kernel, out_shape=jax.ShapeDtypeStruct(out_shape, jn...  90.3 us
    reshape x1, other arithmetic, per_device(): estimate.astype(jnp.float32).reshape(freqs, 2, virtual, cols_here * width)  2.79 us

profile of v3, /device:TPU:0, one launch (start us, length us, event | category | flops | bytes accessed | tf_op | source)
XLA Modules:
  0.0 96.3 jit_solution(16693152149487244916)
XLA Ops:
  0.0 0.8 convert_bitcast_fusion
  0.8 0.9 multiply_bitcast_fusion
  1.7 0.6 fusion.2
  2.4 0.8 fusion.1.cells_right_ref
  3.1 90.3 %shard_map.109 = bf16[16,16,2048]{2,1,0:T(8,128)(2,1)} custom-call(f32[8]{0:T(128)} %levels_ref.1, f32[16]{0:T(128)} %steps_ref.1, bf16[256,256]{1,0:T(8,128)(2,1)} %constant.20.clone.to_high, bf16[256,256]{1,0:T(8,128)(2,1)} %constant.21.clone.to_low, bf16[256,256]{1,0:T(8,128)(2,1)} %constant.22.clone.back_high, bf16[256,256]{1,0:T(8,128)(2,1)} %constant.23.clone.back_low, ...), custom_call_target="tpu_custom_call" | custom-call | tf_op jit(solution)/shard_map/pallas_call | solution.py:591
  93.5 2.8 %bitcast_convert_fusion = f32[16,2,8,2048]{3,2,1,0:T(8,128)} fusion(bf16[16,16,2048]{2,1,0:T(8,128)(2,1)} %shard_map.109), kind=kLoop, calls=%fused_computation | loop fusion | flops 524288 | bytes 3145728 | tf_op jit(solution)/shard_map/reshape | solution.py:629

commit v4 on v3

--- a/solution.py
+++ b/solution.py
@@ -188,7 +188,7 @@
         out_ref[peer, at] = together[:, peer * width : (peer + 1) * width].astype(jnp.bfloat16)
 
 
-def dual_kernel(base, left_ref, recorded_ref, weight_ref, out_ref):
+def dual_kernel(base, all_rows, left_ref, recorded_ref, weight_ref, out_ref):
     freqs, rows, cols, _, rank, width = left_ref.shape
     peers = out_ref.shape[0]
     for at in range(freqs):
@@ -197,11 +197,11 @@
             left_rows = left_ref[at, row].reshape(cols * 2 * rank, width)
             part = recorded_ref[at, :, :, row * width : (row + 1) * width]
             field = part.reshape(-1, width)
-            duals.append(dual_of(left_rows, field, weight_ref[pl.ds((base + at) * rows + row, 1), :], rank))
+            duals.append(dual_of(left_rows, field, weight_ref[pl.ds(base + at * all_rows + row, 1), :], rank))
         store_duals(out_ref, at, duals, peers)
 
 
-def image_kernel(base, left_ref, coefs_ref, recorded_ref, weight_ref, out_ref):
+def image_kernel(base, all_rows, left_ref, coefs_ref, recorded_ref, weight_ref, out_ref):
     freqs, rows, cols, _, rank, width = left_ref.shape
     peers = coefs_ref.shape[0]
     share = cols // peers * 2 * rank
@@ -220,7 +220,7 @@
                 image += nn_dot(both, left_rows[peer * share : (peer + 1) * share])
             part = recorded_ref[at, :, :, row * width : (row + 1) * width]
             field = part.reshape(-1, width) - image
-            duals.append(dual_of(left_rows, field, weight_ref[pl.ds((base + at) * rows + row, 1), :], rank))
+            duals.append(dual_of(left_rows, field, weight_ref[pl.ds(base + at * all_rows + row, 1), :], rank))
         store_duals(out_ref, at, duals, peers)
 
 
@@ -377,7 +377,7 @@
 
 def whole_kernel(
     levels_ref, steps_ref, to_high, to_low, back_high, back_low,
-    left_hbm, right_hbm, recorded_ref, cells_left_ref, cells_right_ref,
+    left_hbm, right_hbm, recorded_ref, ranks_ref, scales_ref,
     out_ref,
     left, right, left_sem, right_sem, weight_left_ref, weight_right_ref,
     tile_send, tile_recv, freq_send, freq_recv, tile_ssem, tile_rsem, freq_ssem, freq_rsem,
@@ -398,6 +398,11 @@
         for n in range(freq_send.shape[0])
     ]
 
+    all_rows = right.shape[2]
+
+    def left_base(at):
+        return at * block * all_rows + lax.axis_index("tile") * left.shape[2]
+
     def span(start):
         return (step >= start) & (step < start + blocks)
 
@@ -430,15 +435,16 @@
                     device_id_type=pl.DeviceIdType.MESH,
                 )
                 count += 1
-        lane_weights(cells_left_ref, weight_left_ref, rank)
-        lane_weights(cells_right_ref, weight_right_ref, rank)
+        lane_weights(ranks_ref, scales_ref, 0, weight_left_ref, rank)
+        first_tile = lax.axis_index("tile") * right.shape[3]
+        lane_weights(ranks_ref, scales_ref, first_tile, weight_right_ref, rank)
         pl.semaphore_wait(barrier, count)
 
     @pl.when(span(0))
     def _():
         fetch(left_hbm, left, left_sem, step).wait()
         dual_kernel(
-            step * block, left.at[step], recorded_ref, weight_left_ref,
+            left_base(step), all_rows, left.at[step], recorded_ref, weight_left_ref,
             over_tile[0].send.at[:, step],
         )
         over_tile[0].start(step)
@@ -480,7 +486,7 @@
         b = step - first_shrink - lag
         over_tile[1].wait(b)
         image_kernel(
-            b * block, left.at[b], over_tile[1].recv.at[:, b], recorded_ref, weight_left_ref,
+            left_base(b), all_rows, left.at[b], over_tile[1].recv.at[:, b], recorded_ref, weight_left_ref,
             over_tile[2].send.at[:, b],
         )
         over_tile[2].start(b)
@@ -516,16 +522,19 @@
 AHEAD = 3
 
 
-def lane_weights(cells_ref, out_ref, rank):
-    _, rows, tiles = cells_ref.shape
+def lane_weights(ranks_ref, scales_ref, first_tile, out_ref, rank):
+    freqs, rows, tiles = ranks_ref.shape
     lanes = out_ref.shape[1]
-    owner = lax.broadcasted_iota(jnp.int32, (tiles, lanes), 1) // (2 * rank)
+    owner = first_tile + lax.broadcasted_iota(jnp.int32, (tiles, lanes), 1) // (2 * rank)
     pick = (owner == lax.broadcasted_iota(jnp.int32, (tiles, lanes), 0)).astype(jnp.float32)
     widen = lambda values: jnp.dot(
-        values, pick, precision=lax.Precision.HIGHEST, preferred_element_type=jnp.float32
+        values.reshape(freqs * rows, tiles), pick, precision=lax.Precision.HIGHEST,
+        preferred_element_type=jnp.float32,
     )
-    slot = (lane_ids(rows, lanes) % rank).astype(jnp.float32)
-    out_ref[...] = jnp.where(slot < widen(cells_ref[0]) - 0.5, widen(cells_ref[1]), 0.0)
+    slot = (lane_ids(freqs * rows, lanes) % rank).astype(jnp.float32)
+    ranks = widen(ranks_ref[...].astype(jnp.float32))
+    scales = widen(scales_ref[:, 0] * scales_ref[:, 1])
+    out_ref[...] = jnp.where(slot < ranks - 0.5, scales, 0.0)
 
 
 def table_parts():
@@ -557,18 +566,9 @@
     tile_size = col_tiles // cols_here
     share = cols_here * 2 * rank
     lines = rows_here * virtual
-    tile_pos = lax.axis_index("tile")
     block = 2 if freqs % 2 == 0 else 1
     blocks = freqs // block
     lag, first_shrink, second_shrink, steps = stages(blocks)
-
-    cells = jnp.stack(
-        [tile_ranks.astype(jnp.float32), tile_scales[:, 0] * tile_scales[:, 1]]
-    )
-    cells_left = lax.dynamic_slice_in_dim(cells, tile_pos * rows_here, rows_here, 2)
-    cells_left = cells_left.reshape(2, freqs * rows_here, col_tiles)
-    cells_right = lax.dynamic_slice_in_dim(cells, tile_pos * cols_here, cols_here, 3)
-    cells_right = cells_right.reshape(2, freqs * row_tiles, cols_here)
 
     def spec(array, index):
         rest = array.shape[1:]
@@ -602,7 +602,7 @@
             pltpu.VMEM((blocks, block) + right_factor.shape[1:], jnp.bfloat16),
             dma((blocks,)),
             dma((blocks,)),
-            pltpu.VMEM((freqs * rows_here, col_tiles * 2 * rank), jnp.float32),
+            pltpu.VMEM((freqs * row_tiles, col_tiles * 2 * rank), jnp.float32),
             pltpu.VMEM((freqs * row_tiles, share), jnp.float32),
             tile_buffer,
             tile_buffer,
@@ -624,7 +624,7 @@
         ),
     )(
         thresholds, step_sizes, *table_parts(), left_factor, right_factor, recorded,
-        cells_left, cells_right,
+        tile_ranks, tile_scales,
     )
     return estimate.astype(jnp.float32).reshape(freqs, 2, virtual, cols_here * width)
 
@@ -639,6 +639,7 @@
         and 128 % (2 * rank) == 0
         and (cols_here * 2 * rank) % 128 == 0
         and arrays[4].shape[2] == 8
+        and right_factor.shape[1] % 8 == 0
         and left_factor.shape[0] * lax.axis_size("freq") == F
     )
     return (per_device if aligned else per_device_plain)(*arrays)

time: 96.5 us -> 93.4 us (0.968)
  other arithmetic: 5.9 us -> 2.79 us
    another operation x2 -> x0, other arithmetic: 1.47 us -> none  [per_device(): jnp.stack([tile_ranks.astype(jnp.float32), tile_scales[:, 0] * tile_scale...]
where the time goes in v4:
time: 93.4 us; the launch traced here: 93.2 us
  Pallas kernels  90.4 us (97%)
  other arithmetic  2.79 us (3%)
    pallas_call x1, Pallas kernels, per_device(): pl.pallas_call(whole_kernel, out_shape=jax.ShapeDtypeStruct(out_shape, jn...  90.4 us
    reshape x1, other arithmetic, per_device(): estimate.astype(jnp.float32).reshape(freqs, 2, virtual, cols_here * width)  2.79 us

profile of v4, /device:TPU:0, one launch (start us, length us, event | category | flops | bytes accessed | tf_op | source)
XLA Modules:
  0.0 93.2 jit_solution(586670932896034919)
XLA Ops:
  0.0 90.4 %shard_map.109 = bf16[16,16,2048]{2,1,0:T(8,128)(2,1)} custom-call(f32[8]{0:T(128)} %levels_ref.1, f32[16]{0:T(128)} %steps_ref.1, bf16[256,256]{1,0:T(8,128)(2,1)} %constant.8.clone.to_high, bf16[256,256]{1,0:T(8,128)(2,1)} %constant.9.clone.to_low, bf16[256,256]{1,0:T(8,128)(2,1)} %constant.10.clone.back_high, bf16[256,256]{1,0:T(8,128)(2,1)} %constant.11.clone.back_low, ...), custom_call_target="tpu_custom_call" | custom-call | tf_op jit(solution)/shard_map/pallas_call | solution.py:591
  90.4 2.8 %bitcast_convert_fusion = f32[16,2,8,2048]{3,2,1,0:T(8,128)} fusion(bf16[16,16,2048]{2,1,0:T(8,128)(2,1)} %shard_map.109), kind=kLoop, calls=%fused_computation | loop fusion | flops 524288 | bytes 3145728 | tf_op jit(solution)/shard_map/reshape | solution.py:629
